TPU v7x, 32 devices: a whole 2x2x4 slice. The times are simulated.
32 devices in a mesh: dp: 8 (over z, x), rep: 4 (over y, core).
Axes of the slice: x: 2, y: 2, z: 4, core: 2. Of those that a mesh axis runs over, the one named last changes fastest.
Arguments:
- tokens: bfloat16 [32, 512, 1024], P(('dp', 'rep')), may hold values from -6 to 6
- segment_ids: int32 [32, 512], P(('dp', 'rep')), may hold values from 0 to 3, never falling along the last dimension, each value on 1 to 256 neighbouring positions
- cotangent: bfloat16 [32, 512, 1024], P(('dp', 'rep')), may hold values from -6 to 6
- norm_in_gain: bfloat16 [1024], P('dp'), may hold values from 0.5 to 1.5
- norm_in_shift: bfloat16 [1024], P('dp'), may hold values from -3 to 3
- qkv_weight: bfloat16 [1024, 3072], P('dp'), may hold values from -0.1875 to 0.1875
- qkv_bias: bfloat16 [3072], P('dp'), may hold values from -3 to 3
- proj_weight: bfloat16 [1024, 1024], P('dp'), may hold values from -1 to 1
- proj_bias: bfloat16 [1024], P('dp'), may hold values from -3 to 3
- norm_mid_gain: bfloat16 [1024], P('dp'), may hold values from 0.5 to 1.5
- norm_mid_shift: bfloat16 [1024], P('dp'), may hold values from -3 to 3
- up_weight: bfloat16 [1024, 4096], P('dp'), may hold values from -0.1875 to 0.1875
- up_bias: bfloat16 [4096], P('dp'), may hold values from -3 to 3
- down_weight: bfloat16 [4096, 1024], P('dp'), may hold values from -0.09375 to 0.09375
- down_bias: bfloat16 [1024], P('dp'), may hold values from -3 to 3
- prefix_table: bfloat16 [10, 1024], replicated, may hold values from -6 to 6
- first_weight: bfloat16 [1024, 800], P(None, 'rep'), may hold values from -0.1875 to 0.1875
- first_bias: bfloat16 [800], P('rep'), may hold values from -3 to 3
- second_weight: bfloat16 [800, 2048], P('rep', 'dp'), may hold values from -0.3125 to 0.3125
- second_bias: bfloat16 [2048], P('dp'), may hold values from -3 to 3
Outputs:
- activations: bfloat16 [32, 512, 1024], P(('dp', 'rep'))
- input_grad: float32 [32, 512, 1024], P(('dp', 'rep'))
- prefix_table_grad: float32 [10, 1024], replicated
- first_weight_grad: float32 [1024, 800], P(None, 'rep')
- first_bias_grad: float32 [800], P('rep')
- second_weight_grad: float32 [800, 2048], P('rep', 'dp')
- second_bias_grad: float32 [2048], P('dp')
- prefix_kv: float32 [10, 2048], replicated
Inputs may be any that keep to these rules, and one draw needn't show every extreme that they name: `segment_ids`: within each packed row of 512 tokens the ids never fall; each id names one run of consecutive tokens, of 1 to 256 tokens, and some run has exactly that many.
All inputs are finite; a program needn't handle non-finite values.
Results may differ from a plain program's by a relative error of at most 0.01.
The roundings to bfloat16 on the way count: a program that leaves them out, or rounds other values in their place, can miss the bound.
Values may be sent and summed in bfloat16 or wider, within the bound.
A program may use at most 192 MiB of HBM per device.

v0:
```python
import jax
import jax.numpy as jnp
from jax import lax
from jax.sharding import PartitionSpec as P

HEAD_DIM = 64


eps_norm = 1e-05
neg_fill = -1e30
highest = lax.Precision.HIGHEST


def layer_norm(values, gain, shift):
    centred = values - jnp.mean(values, axis=-1, keepdims=True)
    variance = jnp.mean(centred * centred, axis=-1, keepdims=True)
    return centred * lax.rsqrt(variance + eps_norm) * gain + shift


def norm_backward(values, gain, upstream):

    def apply_norm(inner):
        return layer_norm(inner, gain, jnp.zeros_like(gain))

    unused, pullback = jax.vjp(apply_norm, values)
    return pullback(upstream)[0]


def gelu_backward(pre_act, upstream):

    def apply_gelu(inner):
        return jax.nn.gelu(inner, approximate=True)

    unused, pullback = jax.vjp(apply_gelu, pre_act)
    return pullback(upstream)[0]


def allowed_self(row_segments, first_row, block_rows):
    query_pos = first_row + jnp.arange(block_rows)
    key_pos = jnp.arange(row_segments.shape[0])
    same_doc = row_segments[:, None] == row_segments[None, :]
    return same_doc & (key_pos[None, :] <= query_pos[:, None])


def block_scores(query_block, key_self, key_prefix, allowed, score_scale):
    row_scores = (
        jnp.einsum("qhd,khd->hqk", query_block, key_self, preferred_element_type=jnp.float32)
        * score_scale
    )
    row_scores = jnp.where(allowed[None], row_scores, neg_fill)
    pre_scores = (
        jnp.einsum("qhd,khd->hqk", query_block, key_prefix, preferred_element_type=jnp.float32)
        * score_scale
    )
    return (row_scores, pre_scores)


def attend(
    queries, key_self, value_self, key_prefix, value_prefix, row_segments, block_rows, score_scale
):
    length = queries.shape[0]

    def one_block(first_row):
        allowed = allowed_self(row_segments, first_row, block_rows)
        row_scores, pre_scores = block_scores(queries, key_self, key_prefix, allowed, score_scale)
        row_max = jnp.maximum(jnp.max(row_scores, axis=-1), jnp.max(pre_scores, axis=-1))[..., None]
        row_exp = jnp.exp(row_scores - row_max)
        pre_exp = jnp.exp(pre_scores - row_max)
        totals = jnp.sum(row_exp, axis=-1, keepdims=True) + jnp.sum(pre_exp, axis=-1, keepdims=True)
        row_probs = (row_exp / totals).astype(jnp.bfloat16)
        pre_probs = (pre_exp / totals).astype(jnp.bfloat16)
        mixed = jnp.einsum(
            "hqk,khd->qhd", row_probs, value_self, preferred_element_type=jnp.float32
        )
        mixed = mixed + jnp.einsum(
            "hqk,khd->qhd", pre_probs, value_prefix, preferred_element_type=jnp.float32
        )
        return (mixed.astype(jnp.bfloat16), (row_max + jnp.log(totals))[..., 0])

    block_starts = jnp.arange(length // block_rows) * block_rows
    mixed, log_totals = lax.map(one_block, block_starts)
    return (mixed.reshape(length, -1), log_totals)


def attend_back(
    queries,
    key_self,
    value_self,
    key_prefix,
    value_prefix,
    row_segments,
    log_totals,
    grad_mixed,
    block_rows,
    score_scale,
):
    length = queries.shape[0]

    def one_block(running, inputs):
        first_row, block_lse = inputs
        allowed = allowed_self(row_segments, first_row, block_rows)
        row_scores, pre_scores = block_scores(queries, key_self, key_prefix, allowed, score_scale)
        row_probs = jnp.exp(row_scores - block_lse[..., None])
        pre_probs = jnp.exp(pre_scores - block_lse[..., None])
        row_dprob = jnp.einsum(
            "qhd,khd->hqk", grad_mixed, value_self, preferred_element_type=jnp.float32
        )
        pre_dprob = jnp.einsum(
            "qhd,khd->hqk", grad_mixed, value_prefix, preferred_element_type=jnp.float32
        )
        row_dot = jnp.sum(row_probs * row_dprob, axis=-1, keepdims=True) + jnp.sum(
            pre_probs * pre_dprob, axis=-1, keepdims=True
        )
        row_dscore = (row_probs * (row_dprob - row_dot)).astype(jnp.bfloat16)
        pre_dscore = (pre_probs * (pre_dprob - row_dot)).astype(jnp.bfloat16)
        grad_query = jnp.einsum(
            "hqk,khd->qhd", row_dscore, key_self, preferred_element_type=jnp.float32
        )
        grad_query = (
            grad_query
            + jnp.einsum("hqk,khd->qhd", pre_dscore, key_prefix, preferred_element_type=jnp.float32)
        ) * score_scale
        key_self_grad, value_self_grad, key_pre_grad, value_pre_grad = running
        key_self_grad = (
            key_self_grad
            + jnp.einsum("hqk,qhd->khd", row_dscore, queries, preferred_element_type=jnp.float32)
            * score_scale
        )
        value_self_grad = value_self_grad + jnp.einsum(
            "hqk,qhd->khd",
            row_probs.astype(jnp.bfloat16),
            grad_mixed,
            preferred_element_type=jnp.float32,
        )
        key_pre_grad = (
            key_pre_grad
            + jnp.einsum("hqk,qhd->khd", pre_dscore, queries, preferred_element_type=jnp.float32)
            * score_scale
        )
        value_pre_grad = value_pre_grad + jnp.einsum(
            "hqk,qhd->khd",
            pre_probs.astype(jnp.bfloat16),
            grad_mixed,
            preferred_element_type=jnp.float32,
        )
        return ((key_self_grad, value_self_grad, key_pre_grad, value_pre_grad), grad_query)

    initial = (
        jnp.zeros(key_self.shape, jnp.float32),
        jnp.zeros(value_self.shape, jnp.float32),
        jnp.zeros(key_prefix.shape, jnp.float32),
        jnp.zeros(value_prefix.shape, jnp.float32),
    )
    block_starts = jnp.arange(length // block_rows) * block_rows
    running, grad_queries = lax.scan(one_block, initial, (block_starts, log_totals))
    return (grad_queries.reshape(length, -1), running)


def shards(
    tokens,
    segment_ids,
    cotangent,
    norm_in_gain,
    norm_in_shift,
    qkv_weight,
    qkv_bias,
    proj_weight,
    proj_bias,
    norm_mid_gain,
    norm_mid_shift,
    up_weight,
    up_bias,
    down_weight,
    down_bias,
    prefix_table,
    first_weight,
    first_bias,
    second_weight,
    second_bias,
):
    gathered = (
        lax.all_gather(norm_in_gain, "dp", axis=0, tiled=True),
        lax.all_gather(norm_in_shift, "dp", axis=0, tiled=True),
        lax.all_gather(qkv_weight, "dp", axis=0, tiled=True),
        lax.all_gather(qkv_bias, "dp", axis=0, tiled=True),
        lax.all_gather(proj_weight, "dp", axis=0, tiled=True),
        lax.all_gather(proj_bias, "dp", axis=0, tiled=True),
        lax.all_gather(norm_mid_gain, "dp", axis=0, tiled=True),
        lax.all_gather(norm_mid_shift, "dp", axis=0, tiled=True),
        lax.all_gather(up_weight, "dp", axis=0, tiled=True),
        lax.all_gather(up_bias, "dp", axis=0, tiled=True),
        lax.all_gather(down_weight, "dp", axis=0, tiled=True),
        lax.all_gather(down_bias, "dp", axis=0, tiled=True),
        lax.all_gather(second_weight, "dp", axis=1, tiled=True),
        lax.all_gather(second_bias, "dp", axis=0, tiled=True),
    )
    (
        gain_in,
        shift_in,
        qkv_full,
        qkv_shift,
        proj_full,
        proj_shift,
        gain_mid,
        shift_mid,
        up_full,
        up_shift,
        down_full,
        down_shift,
        second_full,
        second_shift,
    ) = gathered
    hidden = jnp.tanh(
        jnp.dot(prefix_table, first_weight, preferred_element_type=jnp.float32)
        + first_bias.astype(jnp.float32)
    )
    hidden_low = hidden.astype(jnp.bfloat16)
    prefix_part = jnp.dot(hidden_low, second_full, preferred_element_type=jnp.float32)
    prefix_kv = lax.psum(prefix_part, "rep") + second_shift.astype(jnp.float32)
    prefix_low = prefix_kv.astype(jnp.bfloat16)
    model_width = prefix_table.shape[1]
    prefix_count = prefix_table.shape[0]
    head_count = model_width // HEAD_DIM
    key_prefix = prefix_low[:, :model_width].reshape(prefix_count, head_count, HEAD_DIM)
    value_prefix = prefix_low[:, model_width:].reshape(prefix_count, head_count, HEAD_DIM)
    row_tokens = tokens[0]
    row_segments = segment_ids[0]
    token_values = row_tokens.astype(jnp.float32)
    length = row_tokens.shape[0]
    block_rows = min(length, 512)
    score_scale = HEAD_DIM ** (-0.5)
    normed_in = layer_norm(
        token_values, gain_in.astype(jnp.float32), shift_in.astype(jnp.float32)
    ).astype(jnp.bfloat16)
    packed = (
        jnp.dot(normed_in, qkv_full, preferred_element_type=jnp.float32)
        + qkv_shift.astype(jnp.float32)
    ).astype(jnp.bfloat16)
    queries = packed[:, :model_width].reshape(length, head_count, HEAD_DIM)
    key_self = packed[:, model_width : 2 * model_width].reshape(length, head_count, HEAD_DIM)
    value_self = packed[:, 2 * model_width :].reshape(length, head_count, HEAD_DIM)
    mixed, log_totals = attend(
        queries,
        key_self,
        value_self,
        key_prefix,
        value_prefix,
        row_segments,
        block_rows,
        score_scale,
    )
    residual = (
        token_values
        + jnp.dot(mixed, proj_full, preferred_element_type=jnp.float32)
        + proj_shift.astype(jnp.float32)
    )
    normed_mid = layer_norm(
        residual, gain_mid.astype(jnp.float32), shift_mid.astype(jnp.float32)
    ).astype(jnp.bfloat16)
    pre_act = jnp.dot(normed_mid, up_full, preferred_element_type=jnp.float32) + up_shift.astype(
        jnp.float32
    )
    activated = jax.nn.gelu(pre_act, approximate=True).astype(jnp.bfloat16)
    result = (
        residual
        + jnp.dot(activated, down_full, preferred_element_type=jnp.float32)
        + down_shift.astype(jnp.float32)
    )
    activations = result.astype(jnp.bfloat16)[None]
    cotangent_low = cotangent[0]
    grad_act = jnp.dot(cotangent_low, down_full.T, preferred_element_type=jnp.float32)
    grad_pre = gelu_backward(pre_act, grad_act).astype(jnp.bfloat16)
    grad_mid = jnp.dot(grad_pre, up_full.T, preferred_element_type=jnp.float32)
    grad_resid = cotangent_low.astype(jnp.float32) + norm_backward(
        residual, gain_mid.astype(jnp.float32), grad_mid
    )
    grad_branch = grad_resid.astype(jnp.bfloat16)
    grad_mixed = jnp.dot(grad_branch, proj_full.T, preferred_element_type=jnp.float32).astype(
        jnp.bfloat16
    )
    grad_mixed = grad_mixed.reshape(length, head_count, HEAD_DIM)
    grad_queries, running = attend_back(
        queries,
        key_self,
        value_self,
        key_prefix,
        value_prefix,
        row_segments,
        log_totals,
        grad_mixed,
        block_rows,
        score_scale,
    )
    key_self_grad, value_self_grad, key_pre_grad, value_pre_grad = running
    grad_packed = jnp.concatenate(
        [grad_queries, key_self_grad.reshape(length, -1), value_self_grad.reshape(length, -1)],
        axis=1,
    ).astype(jnp.bfloat16)
    grad_normed = jnp.dot(grad_packed, qkv_full.T, preferred_element_type=jnp.float32)
    input_grad = (
        grad_resid + norm_backward(token_values, gain_in.astype(jnp.float32), grad_normed)
    )[None]
    prefix_grad = jnp.concatenate(
        [key_pre_grad.reshape(prefix_count, -1), value_pre_grad.reshape(prefix_count, -1)], axis=1
    )
    group_total = lax.psum(prefix_grad, "rep")
    owned = lax.psum_scatter(group_total, "dp", scatter_dimension=1, tiled=True)
    hidden_values = hidden_low.astype(jnp.float32)
    second_weight_grad = jnp.dot(
        hidden_values.T, owned, precision=highest, preferred_element_type=jnp.float32
    )
    second_bias_grad = jnp.sum(owned, axis=0)
    hidden_part = jnp.dot(
        owned,
        second_weight.astype(jnp.float32).T,
        precision=highest,
        preferred_element_type=jnp.float32,
    )
    grad_hidden = lax.psum(hidden_part, "dp")
    grad_inner = grad_hidden * (1.0 - hidden * hidden)
    first_weight_grad = jnp.dot(
        prefix_table.astype(jnp.float32).T,
        grad_inner,
        precision=highest,
        preferred_element_type=jnp.float32,
    )
    first_bias_grad = jnp.sum(grad_inner, axis=0)
    table_part = jnp.dot(
        grad_inner,
        first_weight.astype(jnp.float32).T,
        precision=highest,
        preferred_element_type=jnp.float32,
    )
    prefix_table_grad = lax.psum(table_part, "rep")
    return (
        activations,
        input_grad,
        prefix_table_grad,
        first_weight_grad,
        first_bias_grad,
        second_weight_grad,
        second_bias_grad,
        prefix_kv,
    )


def solution(mesh):
    in_specs = (
        P(("dp", "rep"), None, None),
        P(("dp", "rep"), None),
        P(("dp", "rep"), None, None),
        P("dp"),
        P("dp"),
        P("dp", None),
        P("dp"),
        P("dp", None),
        P("dp"),
        P("dp"),
        P("dp"),
        P("dp", None),
        P("dp"),
        P("dp", None),
        P("dp"),
        P(),
        P(None, "rep"),
        P("rep"),
        P("rep", "dp"),
        P("dp"),
    )
    out_specs = (
        P(("dp", "rep"), None, None),
        P(("dp", "rep"), None, None),
        P(),
        P(None, "rep"),
        P("rep"),
        P("rep", "dp"),
        P("dp"),
        P(),
    )
    return jax.shard_map(shards, mesh=mesh, in_specs=in_specs, out_specs=out_specs, check_vma=False)
```

profile of v0, /device:TPU:1, one launch (start us, length us, event | category | flops | bytes accessed | tf_op | source)
XLA Modules:
  0.0 664.1 jit_solution(11809928841672032311)
XLA Ops:
  9.0 28.4 %all_gather.46 = bf16[200,2048]{1,0:T(8,128)(2,1)S(1)} all-gather(bf16[200,256]{1,0:T(8,128)(2,1)} %param.38), channel_id=1, replica_groups=mesh['dp'=8,'rep'=4] {'dp'}, dimensions={1}, use_global_device_ids=true | all-gather | bytes 921600 | tf_op jit(solution)/shard_map/all_gather | solution.py:194
  42.5 16.1 %all-gather = bf16[8,1,128]{2,1,0:T(2,128)(2,1)S(1)} all-gather(bf16[1,1,128]{2,1,0:T(2,128)(2,1)S(1)} %bitcast.156), channel_id=1, replica_groups=mesh['dp'=8,'rep'=4] {'dp'}, dimensions={0}, use_global_device_ids=true | all-gather | bytes 2304 | tf_op jit(solution)/shard_map/all_gather | solution.py:182
  58.6 12.9 %all-gather.1 = bf16[8,1,128]{2,1,0:T(2,128)(2,1)S(1)} all-gather(bf16[1,1,128]{2,1,0:T(2,128)(2,1)S(1)} %bitcast.157), channel_id=1, replica_groups=mesh['dp'=8,'rep'=4] {'dp'}, dimensions={0}, use_global_device_ids=true | all-gather | bytes 2304 | tf_op jit(solution)/shard_map/all_gather | solution.py:183
  71.6 15.1 %all-gather.4 = bf16[8,1,128]{2,1,0:T(2,128)(2,1)S(1)} all-gather(bf16[1,1,128]{2,1,0:T(2,128)(2,1)S(1)} %bitcast.158), channel_id=1, replica_groups=mesh['dp'=8,'rep'=4] {'dp'}, dimensions={0}, use_global_device_ids=true | all-gather | bytes 2304 | tf_op jit(solution)/shard_map/all_gather | solution.py:187
  87.2 12.8 %all-gather.5 = bf16[8,1,128]{2,1,0:T(2,128)(2,1)S(1)} all-gather(bf16[1,1,128]{2,1,0:T(2,128)(2,1)S(1)} %bitcast.159), channel_id=1, replica_groups=mesh['dp'=8,'rep'=4] {'dp'}, dimensions={0}, use_global_device_ids=true | all-gather | bytes 2304 | tf_op jit(solution)/shard_map/all_gather | solution.py:188
  100.6 15.3 %all-gather.6 = bf16[8,1,128]{2,1,0:T(2,128)(2,1)S(1)} all-gather(bf16[1,1,128]{2,1,0:T(2,128)(2,1)S(1)} %bitcast.160), channel_id=1, replica_groups=mesh['dp'=8,'rep'=4] {'dp'}, dimensions={0}, use_global_device_ids=true | all-gather | bytes 2304 | tf_op jit(solution)/shard_map/all_gather | solution.py:189
  116.5 12.8 %all-gather.8 = bf16[8,1,128]{2,1,0:T(2,128)(2,1)S(1)} all-gather(bf16[1,1,128]{2,1,0:T(2,128)(2,1)S(1)} %bitcast.161), channel_id=1, replica_groups=mesh['dp'=8,'rep'=4] {'dp'}, dimensions={0}, use_global_device_ids=true | all-gather | bytes 2304 | tf_op jit(solution)/shard_map/all_gather | solution.py:193
  129.9 15.0 %all-gather.3 = bf16[8,1,256]{2,1,0:T(2,128)(2,1)S(1)} all-gather(bf16[1,1,256]{2,1,0:T(2,128)(2,1)S(1)} %reshape.218), channel_id=1, replica_groups=mesh['dp'=8,'rep'=4] {'dp'}, dimensions={0}, use_global_device_ids=true | all-gather | bytes 4608 | tf_op jit(solution)/shard_map/all_gather | solution.py:195
  144.9 21.5 %all-gather.2 = bf16[8,1,384]{2,1,0:T(2,128)(2,1)S(1)} all-gather(bf16[1,1,384]{2,1,0:T(2,128)(2,1)S(1)} %reshape.216), channel_id=1, replica_groups=mesh['dp'=8,'rep'=4] {'dp'}, dimensions={0}, use_global_device_ids=true | all-gather | bytes 6912 | tf_op jit(solution)/shard_map/all_gather | solution.py:185
  166.5 22.3 %all-gather.7 = bf16[8,1,512]{2,1,0:T(2,128)(2,1)S(1)} all-gather(bf16[1,1,512]{2,1,0:T(2,128)(2,1)S(1)} %reshape.226), channel_id=1, replica_groups=mesh['dp'=8,'rep'=4] {'dp'}, dimensions={0}, use_global_device_ids=true | all-gather | bytes 9216 | tf_op jit(solution)/shard_map/all_gather | solution.py:191
  194.0 6.7 %add_convert_fusion = bf16[512,3072]{1,0:T(8,128)(2,1)S(1)} fusion(bf16[1024,3072]{1,0:T(8,128)(2,1)} %all-gather.14.cloned.1.call-done, f32[3072]{0:T(1024)S(1)} %bitcast.151, bf16[1,512,1024]{2,1,0:T(8,128)(2,1)S(1)} %copy-done.1, f32[1024]{0:T(1024)S(1)} %bitcast.155, f32[1024]{0:T(1024)S(1)} %bitcast.141, f32[512]{0:T(512)S(1)} %fusion.73, ...), kind=kOutput, calls=%fused_computation.21 | convolution fusion | flops 3227516928 | bytes 10510336 | tf_op jit(solution)/shard_map/dot_general | solution.py:236
  204.7 2.3 copy.62
  208.1 8.5 %fusion.93 = (f32[16,512]{1,0:T(8,128)S(1)}, f32[16,512,512]{1,2,0:T(8,128)}) fusion(bf16[512,16,64]{0,2,1:T(8,128)(2,1)S(1)} %bitcast.125, bf16[512,16,64]{0,2,1:T(8,128)(2,1)S(1)} %bitcast.132, pred[512,512]{0,1:T(8,128)(4,1)} %fusion.56), kind=kOutput, calls=%fused_computation.133 | convolution fusion | flops 549445632 | bytes 19169280 | tf_op jit(solution)/shard_map/while/body/eval_jaxpr/qhd,khd->hqk/dot_general | solution.py:47
  216.9 8.4 %fusion = f32[16,512]{1,0:T(8,128)S(1)} fusion(f32[16,512,512]{1,2,0:T(8,128)} %get-tuple-element.75, f32[16,512]{1,0:T(8,128)S(1)} %max.12), kind=kLoop, calls=%fused_computation.6 | loop fusion | flops 8380416 | bytes 16842752 | tf_op jit(solution)/shard_map/while/body/eval_jaxpr/reduce_sum | solution.py:69
  225.9 7.7 %fusion.12 = f32[16,64,512]{2,1,0:T(8,128)S(1)} fusion(bf16[512,16,64]{0,2,1:T(8,128)(2,1)S(1)} %bitcast.134, f32[16,512,512]{1,2,0:T(8,128)} %get-tuple-element.75, f32[16,512]{1,0:T(8,128)S(1)} %get-tuple-element.64, f32[16,512]{1,0:T(8,128)S(1)} %max.12), kind=kOutput, calls=%fused_computation.20 | convolution fusion | flops 549453824 | bytes 19988480 | tf_op jit(solution)/shard_map/while/body/eval_jaxpr/hqk,khd->qhd/dot_general | solution.py:72
  235.0 3.0 fusion.95
  240.8 81.4 %all-gather.18.cloned.1.call-done = bf16[1024,4096]{1,0:T(8,128)(2,1)} async-done(((bf16[128,4096]{1,0:T(8,128)(2,1)}), bf16[1024,4096]{1,0:T(8,128)(2,1)}) %all-gather.18.cloned.1.call-update) | async-done | bytes 8388624 | tf_op jit(solution)/shard_map/all_gather | solution.py:190
  322.2 12.3 %fusion.42 = f32[512,4096]{1,0:T(8,128)} fusion(bf16[1024,4096]{1,0:T(8,128)(2,1)} %all-gather.18.cloned.1.call-done, f32[512,1024]{1,0:T(8,128)} %copy-done.2, f32[1024]{0:T(1024)} %bitcast.154, f32[1024]{0:T(1024)} %bitcast.148, f32[512]{0:T(512)} %fusion.74, f32[512]{0:T(512)} %copy-done.36), kind=kOutput, calls=%fused_computation.66 | convolution fusion | flops 4297588736 | bytes 18886656 | tf_op jit(solution)/shard_map/dot_general | solution.py:260
  334.5 112.8 %all-gather.20.cloned.1.call-done = bf16[4096,1024]{1,0:T(8,128)(2,1)} async-done(((bf16[512,1024]{1,0:T(8,128)(2,1)}), bf16[4096,1024]{1,0:T(8,128)(2,1)}) %all-gather.20.cloned.1.call-update) | async-done | bytes 8388624 | tf_op jit(solution)/shard_map/all_gather | solution.py:192
  447.3 18.3 %multiply_reduce_fusion.1 = (f32[512]{0:T(512)}, f32[512,1024]{1,0:T(8,128)}) fusion(f32[512,1024]{1,0:T(8,128)} %copy-done.2, f32[1024]{0:T(1024)} %bitcast.149, f32[512]{0:T(512)} %copy-done.36, bf16[1024,4096]{1,0:T(8,128)(2,1)} %all-gather.18.cloned.1.call-done, f32[512,4096]{1,0:T(8,128)} %fusion.42, f32[4096]{0:T(1024)} %bitcast.146, ...), kind=kOutput, calls=%fused_computation.50 | convolution fusion | flops 8636071936 | bytes 30433280 | tf_op jit(solution)/shard_map/dot_general | solution.py:273
  466.2 3.0 fusion.89
  477.2 9.5 %fusion.34 = bf16[16,64,512]{2,1,0:T(8,128)(2,1)} fusion(bf16[512,16,64]{0,2,1:T(8,128)(2,1)S(1)} %bitcast.130, f32[16,512,512]{1,2,0:T(8,128)} %get-tuple-element.75, f32[16,512]{1,0:T(8,128)S(1)} %copy-done.13), kind=kOutput, calls=%fused_computation.56 | convolution fusion | flops 545783808 | bytes 18907136 | tf_op jit(solution)/shard_map/while/body/eval_jaxpr/hqk,qhd->khd/dot_general | solution.py:129
  486.7 11.2 %multiply_reduce_fusion = (f32[16,512]{1,0:T(8,128)S(1)}, f32[16,512,512]{1,2,0:T(8,128)}) fusion(f32[16,512,512]{1,2,0:T(8,128)} %get-tuple-element.75, f32[16,512]{1,0:T(8,128)S(1)} %copy-done.13, bf16[512,16,64]{0,2,1:T(8,128)(2,1)S(1)} %bitcast.131, bf16[512,16,64]{0,2,1:T(8,128)(2,1)S(1)} %bitcast.135), kind=kOutput, calls=%fused_computation.1 | convolution fusion | flops 549445632 | bytes 35717120 | tf_op jit(solution)/shard_map/while/body/eval_jaxpr/qhd,khd->hqk/dot_general | solution.py:105
  501.1 25.0 %multiply_convert_fusion = bf16[16,512,512]{1,2,0:T(8,128)(2,1)} fusion(f32[16,512,512]{1,2,0:T(8,128)} %get-tuple-element.97, f32[16,512,512]{1,2,0:T(8,128)} %get-tuple-element.75, f32[16,512]{1,0:T(8,128)S(1)} %add.206, f32[16,512]{1,0:T(8,128)S(1)} %copy-done.14), kind=kLoop, calls=%fused_computation | loop fusion | flops 16777216 | bytes 42008576 | tf_op jit(solution)/shard_map/while/body/eval_jaxpr/convert_element_type | solution.py:114
  526.8 7.1 %multiply_convert_fusion.3 = bf16[16,64,512]{2,1,0:T(8,128)(2,1)} fusion(bf16[512,16,64]{0,2,1:T(8,128)(2,1)S(1)} %bitcast.127, bf16[16,512,512]{1,2,0:T(8,128)(2,1)} %multiply_convert_fusion), kind=kOutput, calls=%fused_computation.47 | convolution fusion | flops 537919488 | bytes 10485760 | tf_op jit(solution)/shard_map/while/body/eval_jaxpr/hqk,qhd->khd/dot_general | solution.py:126
  534.7 5.6 multiply_convert_fusion.4
  540.4 6.8 %fusion.32 = (f32[512]{0:T(512)S(1)}, f32[512,1024]{1,0:T(8,128)S(1)}) fusion(bf16[1,512,1024]{2,1,0:T(8,128)(2,1)S(1)} %copy-done.1, f32[1024]{0:T(1024)S(1)} %bitcast.142, f32[512]{0:T(512)S(1)} %copy-done.31, bf16[1024,3072]{1,0:T(8,128)(2,1)} %all-gather.14.cloned.1.call-done, bf16[512,1024]{0,1:T(8,128)(2,1)S(1)} %bitcast.138, ...), kind=kOutput, calls=%fused_computation.44 | convolution fusion | flops 3233283584 | bytes 12591104 | tf_op jit(solution)/shard_map/dot_general | solution.py:299
  548.8 10.2 %fusion.37 = bf16[1,512,1024]{2,1,0:T(8,128)(2,1)} fusion(f32[512,1024]{1,0:T(8,128)S(1)} %copy-done.3, bf16[4096,1024]{1,0:T(8,128)(2,1)S(1)} %bitcast.163, f32[512,4096]{1,0:T(8,128)} %fusion.42, f32[4096]{0:T(1024)S(1)} %bitcast.147, f32[1024]{0:T(1024)S(1)} %bitcast.153), kind=kOutput, calls=%fused_computation.57 | convolution fusion | flops 4317511680 | bytes 19943424 | tf_op jit(solution)/shard_map/dot_general | solution.py:266
  561.3 31.6 %reduce-scatter.2.cloned.1.call-done = f32[10,256]{1,0:T(8,128)} async-done(((f32[10,2048]{1,0:T(8,128)}), f32[10,256]{1,0:T(8,128)}) %reduce-scatter.2.cloned.1.call-update) | async-done | bytes 10256 | tf_op jit(solution)/shard_map/reduce_scatter | solution.py:307
  592.9 12.3 %psum.32 = f32[10,256]{1,0:T(8,128)S(1)} all-reduce(f32[10,256]{1,0:T(8,128)} %reduce-scatter.2.cloned.1.call-done), channel_id=1, replica_groups=mesh['dp'=8,'rep'=4] {'rep'}, use_global_device_ids=true, to_apply=%region_15.16 | all-reduce | flops 2560 | bytes 20480 | tf_op jit(solution)/shard_map/psum | solution.py:306
  605.3 28.0 %psum.30 = f32[10,200]{1,0:T(8,128)S(1)} all-reduce(f32[10,200]{1,0:T(8,128)S(1)} %fusion.96), channel_id=1, replica_groups=mesh['dp'=8,'rep'=4] {'dp'}, use_global_device_ids=true, to_apply=%region_17.18 | all-reduce | flops 2000 | bytes 16000 | tf_op jit(solution)/shard_map/psum | solution.py:319
  637.2 19.0 %psum.31 = f32[10,1024]{1,0:T(8,128)} all-reduce(f32[10,1024]{1,0:T(8,128)S(1)} %fusion.87), channel_id=1, replica_groups=mesh['dp'=8,'rep'=4] {'rep'}, use_global_device_ids=true, to_apply=%region_18.19 | all-reduce | flops 10240 | bytes 81920 | tf_op jit(solution)/shard_map/psum | solution.py:334
  (184 shorter events, 44.5 us)
Async XLA Ops:
  8.0 29.4 %copy-start = (bf16[1024,200]{0,1:T(8,128)(2,1)S(1)}, bf16[1024,200]{0,1:T(8,128)(2,1)}, u32[]{:S(2)}) copy-start(bf16[1024,200]{0,1:T(8,128)(2,1)} %param.36) | copy-start | bytes 1228804
  8.0 34.5 %copy-start.51 = (bf16[256]{0:T(256)(128)(2,1)S(1)}, bf16[256]{0:T(256)(128)(2,1)}, u32[]{:S(2)}) copy-start(bf16[256]{0:T(256)(128)(2,1)} %param.39) | copy-start | bytes 1540
  8.0 34.5 %copy-start.44 = (bf16[384]{0:T(512)(128)(2,1)S(1)}, bf16[384]{0:T(512)(128)(2,1)}, u32[]{:S(2)}) copy-start(bf16[384]{0:T(512)(128)(2,1)} %param.26) | copy-start | bytes 2308
  8.0 34.5 %copy-start.43 = (bf16[512]{0:T(512)(128)(2,1)S(1)}, bf16[512]{0:T(512)(128)(2,1)}, u32[]{:S(2)}) copy-start(bf16[512]{0:T(512)(128)(2,1)} %param.32) | copy-start | bytes 3076
  8.0 34.5 %copy-start.45 = (bf16[128]{0:T(256)(128)(2,1)S(1)}, bf16[128]{0:T(256)(128)(2,1)}, u32[]{:S(2)}) copy-start(bf16[128]{0:T(256)(128)(2,1)} %param.23) | copy-start | bytes 772
  8.1 50.6 %copy-start.46 = (bf16[128]{0:T(256)(128)(2,1)S(1)}, bf16[128]{0:T(256)(128)(2,1)}, u32[]{:S(2)}) copy-start(bf16[128]{0:T(256)(128)(2,1)} %param.24) | copy-start | bytes 772
  8.1 63.5 %copy-start.47 = (bf16[128]{0:T(256)(128)(2,1)S(1)}, bf16[128]{0:T(256)(128)(2,1)}, u32[]{:S(2)}) copy-start(bf16[128]{0:T(256)(128)(2,1)} %param.28) | copy-start | bytes 772
  8.1 79.2 %copy-start.48 = (bf16[128]{0:T(256)(128)(2,1)S(1)}, bf16[128]{0:T(256)(128)(2,1)}, u32[]{:S(2)}) copy-start(bf16[128]{0:T(256)(128)(2,1)} %param.29) | copy-start | bytes 772
  8.1 92.5 %copy-start.49 = (bf16[128]{0:T(256)(128)(2,1)S(1)}, bf16[128]{0:T(256)(128)(2,1)}, u32[]{:S(2)}) copy-start(bf16[128]{0:T(256)(128)(2,1)} %param.30) | copy-start | bytes 772
  8.1 108.4 %copy-start.50 = (bf16[128]{0:T(256)(128)(2,1)S(1)}, bf16[128]{0:T(256)(128)(2,1)}, u32[]{:S(2)}) copy-start(bf16[128]{0:T(256)(128)(2,1)} %param.34) | copy-start | bytes 772
  8.1 181.3 %copy-start.1 = (bf16[1,512,1024]{2,1,0:T(8,128)(2,1)S(1)}, bf16[1,512,1024]{2,1,0:T(8,128)(2,1)}, u32[]{:S(2)}) copy-start(bf16[1,512,1024]{2,1,0:T(8,128)(2,1)} %param.20) | copy-start | bytes 3145732
  8.1 182.8 %all-reduce.2.cloned.1.call-start = ((), (), s32[]{:S(2)}) async-start(), calls=%async_computation.2 | async-start | bytes 262144 | tf_op jit(solution)/shard_map/psum | solution.py:219
  39.0 151.0 %copy-start.39 = (s32[1,512]{1,0:T(1,128)S(1)}, s32[1,512]{1,0:T(1,128)}, u32[]{:S(2)}) copy-start(s32[1,512]{1,0:T(1,128)} %param.21) | copy-start | bytes 6148
  39.9 154.0 %all-gather.14.cloned.1.call-start = ((), (), s32[]{:S(2)}) async-start(), calls=%async_computation.1 | async-start | bytes 7077888 | tf_op jit(solution)/shard_map/all_gather | solution.py:184
  40.5 194.4 %all-gather.16.cloned.1.call-start = ((), (), s32[]{:S(2)}) async-start(), calls=%async_computation.3 | async-start | bytes 2359296 | tf_op jit(solution)/shard_map/all_gather | solution.py:186
  41.1 281.1 %all-gather.18.cloned.1.call-start = ((), (), s32[]{:S(2)}) async-start(), calls=%async_computation.4 | async-start | bytes 9437184 | tf_op jit(solution)/shard_map/all_gather | solution.py:190
  41.7 405.6 %all-gather.20.cloned.1.call-start = ((), (), s32[]{:S(2)}) async-start(), calls=%async_computation.5 | async-start | bytes 9437184 | tf_op jit(solution)/shard_map/all_gather | solution.py:192
  42.4 550.5 %reduce-scatter.2.cloned.1.call-start = ((), (), s32[]{:S(2)}) async-start(), calls=%async_computation.6 | async-start | bytes 147456 | tf_op jit(solution)/shard_map/reduce_scatter | solution.py:307
  58.6 135.3 %copy-start.28 = (f32[8,1,128]{2,1,0:T(1,128)}, f32[8,1,128]{2,1,0:T(1,128)S(1)}, u32[]{:S(2)}) copy-start(f32[8,1,128]{2,1,0:T(1,128)S(1)} %convert_element_type.138) | copy-start | bytes 12292
  202.8 13.8 %copy-start.6 = (bf16[512,1024]{0,1:T(8,128)(2,1)}, bf16[512,1024]{0,1:T(8,128)(2,1)S(1)}, u32[]{:S(2)}) copy-start(bf16[512,1024]{0,1:T(8,128)(2,1)S(1)} %copy.64) | copy-start | bytes 3145732
  208.1 25.5 %copy-start.4 = (f32[16,512,10]{1,2,0:T(8,128)}, f32[16,512,10]{1,2,0:T(8,128)S(1)}, u32[]{:S(2)}) copy-start(f32[16,512,10]{1,2,0:T(8,128)S(1)} %get-tuple-element.77) | copy-start | bytes 983044
  216.7 9.2 %copy-start.19 = (f32[16,512]{1,0:T(8,128)}, f32[16,512]{1,0:T(8,128)S(1)}, u32[]{:S(2)}) copy-start(f32[16,512]{1,0:T(8,128)S(1)} %max.12) | copy-start | bytes 98308
  322.2 125.1 %copy-start.15 = (bf16[1,512,1024]{2,1,0:T(8,128)(2,1)S(1)}, bf16[1,512,1024]{2,1,0:T(8,128)(2,1)}, u32[]{:S(2)}) copy-start(bf16[1,512,1024]{2,1,0:T(8,128)(2,1)} %param.22) | copy-start | bytes 3145732
  477.2 9.5 %copy-start.11 = (bf16[512,1024]{0,1:T(8,128)(2,1)S(1)}, bf16[512,1024]{0,1:T(8,128)(2,1)}, u32[]{:S(2)}) copy-start(bf16[512,1024]{0,1:T(8,128)(2,1)} %copy.62) | copy-start | bytes 3145732
  486.7 11.2 %copy-start.5 = (f32[16,512,10]{1,2,0:T(8,128)S(1)}, f32[16,512,10]{1,2,0:T(8,128)}, u32[]{:S(2)}) copy-start(f32[16,512,10]{1,2,0:T(8,128)} %copy-done.4) | copy-start | bytes 983044
  486.7 11.8 %copy-start.20 = (bf16[10,16,64]{2,1,0:T(8,128)(2,1)S(1)}, bf16[10,16,64]{2,1,0:T(8,128)(2,1)}, u32[]{:S(2)}) copy-start(bf16[10,16,64]{2,1,0:T(8,128)(2,1)} %reshape.203) | copy-start | bytes 61444
  548.8 10.2 %copy-start.9 = (f32[512,1024]{1,0:T(8,128)S(1)}, f32[512,1024]{1,0:T(8,128)}, u32[]{:S(2)}) copy-start(f32[512,1024]{1,0:T(8,128)} %copy-done.8) | copy-start | bytes 6291460
  548.8 10.2 %copy-start.16 = (bf16[1,512,1024]{2,1,0:T(8,128)(2,1)S(1)}, bf16[1,512,1024]{2,1,0:T(8,128)(2,1)}, u32[]{:S(2)}) copy-start(bf16[1,512,1024]{2,1,0:T(8,128)(2,1)} %param.22) | copy-start | bytes 3145732
  548.8 10.2 %copy-start.41 = (f32[512]{0:T(512)S(1)}, f32[512]{0:T(512)}, u32[]{:S(2)}) copy-start(f32[512]{0:T(512)} %copy-done.40) | copy-start | bytes 6148
  559.0 46.2 %copy-start.24 = (bf16[200,256]{1,0:T(8,128)(2,1)S(1)}, bf16[200,256]{1,0:T(8,128)(2,1)}, u32[]{:S(2)}) copy-start(bf16[200,256]{1,0:T(8,128)(2,1)} %param.38) | copy-start | bytes 307204
  559.0 74.3 %copy-start.23 = (f32[10,200]{1,0:T(8,128)S(1)}, f32[10,200]{1,0:T(8,128)}, u32[]{:S(2)}) copy-start(f32[10,200]{1,0:T(8,128)} %copy-done.22) | copy-start | bytes 24004
  559.0 76.2 %copy-start.27 = (bf16[10,1024]{1,0:T(8,128)(2,1)S(1)}, bf16[10,1024]{1,0:T(8,128)(2,1)}, u32[]{:S(2)}) copy-start(bf16[10,1024]{1,0:T(8,128)(2,1)} %param.35) | copy-start | bytes 61444
  (28 other events, 123.3 us)
Sparse Core Ops, SparseCore 0:
  40.1 36.2 all-reduce.1
Sparse Core Ops, SparseCore 1:
  42.6 104.0 all-gather.13
  148.9 46.5 all-gather.15
  197.7 124.4 all-gather.17
  324.6 122.7 all-gather.19
  534.7 58.1 reduce-scatter.1
where the time goes:
time: 669 us; the launch traced here: 664 us
  blocking collectives  232 us (35%)
  waiting for transfers between devices  228 us (34%)
  matrix products  121 us (18%)
  other arithmetic  50.9 us (8%)
  between operations  16.6 us (2%)
  local copies, waits for them, and re-layouts  15.6 us (2%)
    all_gather x1, waiting for transfers between devices, shards(): lax.all_gather(down_weight, 'dp', axis=0, tiled=True)  113 us
    all_gather x1, waiting for transfers between devices, shards(): lax.all_gather(up_weight, 'dp', axis=0, tiled=True)  81.4 us
    reduce_scatter x1, waiting for transfers between devices, shards(): owned = lax.psum_scatter(group_total, 'dp', scatter_dimension=1, tiled=True)  31.6 us
    all_gather x1, blocking collectives, shards(): lax.all_gather(second_weight, 'dp', axis=1, tiled=True)  28.4 us
    psum x1, blocking collectives, shards(): grad_hidden = lax.psum(hidden_part, 'dp')  28 us
    convert_element_type x1, other arithmetic, one_block(): row_dscore = (row_probs * (row_dprob - row_dot)).astype(jnp.bfloat16)  25 us
    all_gather x1, blocking collectives, shards(): lax.all_gather(up_bias, 'dp', axis=0, tiled=True)  22.3 us
    all_gather x1, blocking collectives, shards(): lax.all_gather(qkv_bias, 'dp', axis=0, tiled=True)  21.5 us
  transfers between devices with their start and end apart: 6, of which 3 were waited for; matrix products, arithmetic and copies ran while one was open for 14% of the time, Pallas kernels for 0%

commit v1 on v0

v1 whole, which is shorter than its diff:
```python
import functools

import jax
import jax.numpy as jnp
from jax import lax
from jax.experimental import pallas as pl
from jax.experimental.pallas import tpu as pltpu
from jax.sharding import PartitionSpec as P

HEAD_DIM = 64
PAIR = 2 * HEAD_DIM
SLOT = 512
PAD = 16

eps_norm = 1e-05
neg_fill = -1e30
highest = lax.Precision.HIGHEST
f32 = jnp.float32
bf16 = jnp.bfloat16

NN = (((1,), (0,)), ((), ()))
NT = (((1,), (1,)), ((), ()))
TN = (((0,), (0,)), ((), ()))


def mm(left, right, dims=NN):
    return lax.dot_general(left, right, dims, preferred_element_type=f32)


def normalise(values):
    centred = values - jnp.mean(values, axis=-1, keepdims=True)
    variance = jnp.mean(centred * centred, axis=-1, keepdims=True)
    inverse = lax.rsqrt(variance + eps_norm)
    return centred * inverse, inverse


def norm_backward(values, gain, upstream):
    unit, inverse = normalise(values)
    scaled = upstream * gain
    return inverse * (
        scaled
        - jnp.mean(scaled, axis=-1, keepdims=True)
        - unit * jnp.mean(scaled * unit, axis=-1, keepdims=True)
    )


def block_kernel(
    shards,
    prefix_count,
    tokens_hbm,
    cotangent_hbm,
    seg_col,
    seg_row,
    vec_ref,
    prefix_ref,
    weights_hbm,
    activations_hbm,
    input_grad_hbm,
    prefix_grad_ref,
    weights,
    tok,
    cot,
    normed,
    packed,
    keys_t,
    values_t,
    probs,
    bias_t,
    key_pre,
    value_pre,
    pre_f32,
    pre_probs,
    pre_dscore,
    mixed_t,
    acc_a,
    acc_g,
    resid,
    attended,
    grad_packed,
    sem,
    wsem,
):
    length, width = tok.shape
    heads = width // HEAD_DIM
    unit = width // shards
    half = width // SLOT
    scale = HEAD_DIM ** (-0.5)
    group = shards // half

    copies = [
        pltpu.make_async_copy(tokens_hbm, tok, sem.at[0]),
        pltpu.make_async_copy(cotangent_hbm, cot, sem.at[1]),
    ]
    for c in copies:
        c.start()
    blocks = 12
    loads = [
        pltpu.make_async_copy(
            weights_hbm.at[:, pl.ds(b * unit, unit), :],
            weights.at[:, pl.ds(b * unit, unit), :],
            wsem.at[b],
        )
        for b in range(blocks)
    ]
    for c in loads:
        c.start()

    def in_weight(block, col):
        return weights[:, pl.ds(block * unit, unit), pl.ds(col, SLOT)].reshape(width, SLOT)

    def out_weight(block, c):
        return weights[pl.ds(c * group, group), pl.ds(block * unit, unit), :].reshape(SLOT, width)

    def vec(row, col=0, size=None):
        return vec_ref[pl.ds(row, 1), pl.ds(col, width if size is None else size)]

    rows_step = 128
    row_steps = length // rows_step

    copies[0].wait()

    @pl.loop(0, row_steps)
    def _(r):
        rows = pl.ds(r * rows_step, rows_step)
        unit_rows, _ = normalise(tok[rows, :].astype(f32))
        normed[rows, :] = (unit_rows * vec(0) + vec(1)).astype(bf16)
        key_pos = lax.broadcasted_iota(jnp.int32, (rows_step, length), 0) + r * rows_step
        query_pos = lax.broadcasted_iota(jnp.int32, (rows_step, length), 1)
        allowed = (seg_col[rows, :] == seg_row[...]) & (key_pos <= query_pos)
        bias_t[rows, :] = jnp.where(allowed, 0.0, neg_fill)

    head_of_row = lax.broadcasted_iota(jnp.int32, (heads * PAD, width), 0) // PAD
    head_of_col = lax.broadcasted_iota(jnp.int32, (heads * PAD, width), 1) // HEAD_DIM
    own_head = head_of_row == head_of_col
    zero = jnp.zeros((), bf16)
    key_pre[...] = jnp.where(
        own_head, jnp.concatenate([prefix_ref[:, :width]] * heads, axis=0), zero
    )
    value_pre[...] = jnp.where(
        own_head, jnp.concatenate([prefix_ref[:, width:]] * heads, axis=0), zero
    )

    for b in range(3):
        loads[b].wait()

    @pl.loop(0, 3 * half)
    def _(s):
        block = s // half
        col = (s % half) * SLOT
        out = mm(normed[...], in_weight(block, col)) + vec(2 + block, col, SLOT)
        factor = jnp.where(block == 0, scale, 1.0).astype(bf16)
        packed[:, pl.ds(s * SLOT, SLOT)] = out.astype(bf16) * factor

    queries = slice(0, width)
    pre_scores = mm(key_pre[...], packed[:, queries], NT)
    pad_row = lax.broadcasted_iota(jnp.int32, pre_scores.shape, 0) % PAD
    pre_f32[...] = jnp.where(pad_row < prefix_count, pre_scores, neg_fill)

    q_blocks = ((0, length // 2, length // 2), (length // 2, length // 2, length))
    lane_head = lax.broadcasted_iota(jnp.int32, (length, PAIR), 1) // HEAD_DIM

    @pl.loop(0, heads // 2)
    def _(p):
        col = pl.multiple_of(p * PAIR, PAIR)
        q_pair = packed[:, pl.ds(col, PAIR)]
        k_pair = packed[:, pl.ds(width + col, PAIR)]
        v_pair = packed[:, pl.ds(2 * width + col, PAIR)]
        keys_t[pl.ds(col, PAIR), :] = k_pair.T
        values_t[pl.ds(col, PAIR), :] = v_pair.T
        for e in range(2):
            k_head = jnp.where(lane_head == e, k_pair, zero)
            head = 2 * p + e
            feat = pl.ds(pl.multiple_of(head * HEAD_DIM, HEAD_DIM), HEAD_DIM)
            pre_rows = pl.ds(pl.multiple_of(head * PAD, PAD), PAD)
            for q0, q_size, k_size in q_blocks:
                s = mm(k_head[:k_size], q_pair[q0 : q0 + q_size], NT)
                s = s + bias_t[:k_size, q0 : q0 + q_size]
                sp = pre_f32[pre_rows, q0 : q0 + q_size]
                top = jnp.maximum(
                    jnp.max(s, axis=0, keepdims=True), jnp.max(sp, axis=0, keepdims=True)
                )
                s = jnp.exp(s - top)
                sp = jnp.exp(sp - top)
                inverse = 1.0 / (
                    jnp.sum(s, axis=0, keepdims=True) + jnp.sum(sp, axis=0, keepdims=True)
                )
                own = (s * inverse).astype(bf16)
                probs[head, :k_size, q0 : q0 + q_size] = own
                pre_probs[pre_rows, q0 : q0 + q_size] = (sp * inverse).astype(bf16)
                mixed_t[feat, q0 : q0 + q_size] = mm(values_t[feat, :k_size], own)

    @pl.loop(0, width // 128)
    def _(i):
        rows = pl.ds(pl.multiple_of(i * 128, 128), 128)
        full = mixed_t[rows, :] + mm(value_pre[:, rows], pre_probs[...], TN)
        attended[:, rows] = full.T.astype(bf16)

    loads[3].wait()

    @pl.loop(0, half)
    def _(c):
        cols = pl.ds(pl.multiple_of(c * SLOT, SLOT), SLOT)
        out = mm(attended[...], in_weight(3, c * SLOT)) + vec(5, c * SLOT, SLOT)
        resid[:, cols] = tok[:, cols].astype(f32) + out

    @pl.loop(0, row_steps)
    def _(r):
        rows = pl.ds(r * rows_step, rows_step)
        unit_rows, _ = normalise(resid[rows, :])
        normed[rows, :] = (unit_rows * vec(6) + vec(7)).astype(bf16)

    for b in range(4, 12):
        loads[b].wait()
    copies[1].wait()

    ff_steps = 4 * half
    root = 0.7978845608028654
    cube = 0.044715

    @pl.loop(0, ff_steps)
    def _(i):
        col = (i % half) * SLOT
        w_up = in_weight(4 + i // half, col)
        w_down = weights[
            pl.ds(i * (shards // ff_steps), shards // ff_steps), pl.ds(8 * unit, 4 * unit), :
        ].reshape(SLOT, width)
        pre = mm(normed[...], w_up) + vec(8 + i // half, col, SLOT)
        square = pre * pre
        t = jnp.tanh(root * (pre + cube * (square * pre)))
        act = (0.5 * pre * (1.0 + t)).astype(bf16)
        slope = 0.5 * (1.0 + t) + (0.5 * root) * pre * (1.0 - t * t) * (
            1.0 + (3.0 * cube) * square
        )
        grad_act = mm(cot[...], w_down, NT)
        grad_pre = (grad_act * slope).astype(bf16)
        out = mm(act, w_down)
        mid = mm(grad_pre, w_up, NT)

        @pl.when(i == 0)
        def _():
            acc_a[...] = out
            acc_g[...] = mid

        @pl.when(i > 0)
        def _():
            acc_a[...] += out
            acc_g[...] += mid

    @pl.loop(0, row_steps)
    def _(r):
        rows = pl.ds(r * rows_step, rows_step)
        attended[rows, :] = (resid[rows, :] + acc_a[rows, :] + vec(12)).astype(bf16)
        grad = cot[rows, :].astype(f32) + norm_backward(resid[rows, :], vec(6), acc_g[rows, :])
        acc_g[rows, :] = grad
        normed[rows, :] = grad.astype(bf16)

    out_copy = pltpu.make_async_copy(attended, activations_hbm, sem.at[2])
    out_copy.start()
    for c in range(half):
        cot[:, c * SLOT : (c + 1) * SLOT] = mm(normed[...], out_weight(3, c), NT).astype(bf16)
    pre_f32[...] = mm(value_pre[...], cot[...], NT)

    @pl.loop(0, heads // 2)
    def _(p):
        col = pl.multiple_of(p * PAIR, PAIR)
        q_pair = packed[:, pl.ds(col, PAIR)]
        v_pair = packed[:, pl.ds(2 * width + col, PAIR)]
        g_pair = cot[:, pl.ds(col, PAIR)]
        key_grad = jnp.zeros((length, PAIR), f32)
        value_grad = jnp.zeros((length, PAIR), f32)
        for e in range(2):
            own_lanes = lane_head == e
            v_head = jnp.where(own_lanes, v_pair, zero)
            q_head = jnp.where(own_lanes, q_pair, zero)
            g_head = jnp.where(own_lanes, g_pair, zero)
            head = 2 * p + e
            feat = pl.ds(pl.multiple_of(head * HEAD_DIM, HEAD_DIM), HEAD_DIM)
            pre_rows = pl.ds(pl.multiple_of(head * PAD, PAD), PAD)
            for q0, q_size, k_size in q_blocks:
                dp = mm(v_head[:k_size], g_pair[q0 : q0 + q_size], NT)
                own_low = probs[head, :k_size, q0 : q0 + q_size]
                own = own_low.astype(f32)
                pre = pre_probs[pre_rows, q0 : q0 + q_size].astype(f32)
                pre_dp = pre_f32[pre_rows, q0 : q0 + q_size]
                dot = jnp.sum(own * dp, axis=0, keepdims=True) + jnp.sum(
                    pre * pre_dp, axis=0, keepdims=True
                )
                ds = (own * (dp - dot)).astype(bf16)
                pre_dscore[pre_rows, q0 : q0 + q_size] = (pre * (pre_dp - dot)).astype(bf16)
                mixed_t[feat, q0 : q0 + q_size] = mm(keys_t[feat, :k_size], ds)
                dk = mm(ds, q_head[q0 : q0 + q_size])
                dv = mm(own_low, g_head[q0 : q0 + q_size])
                if k_size < length:
                    fill = jnp.zeros((length - k_size, PAIR), f32)
                    dk = jnp.concatenate([dk, fill], axis=0)
                    dv = jnp.concatenate([dv, fill], axis=0)
                key_grad = key_grad + dk
                value_grad = value_grad + dv
        grad_packed[:, pl.ds(width + col, PAIR)] = key_grad.astype(bf16)
        grad_packed[:, pl.ds(2 * width + col, PAIR)] = value_grad.astype(bf16)

    @pl.loop(0, width // 128)
    def _(i):
        rows = pl.ds(pl.multiple_of(i * 128, 128), 128)
        full = mixed_t[rows, :] + mm(key_pre[:, rows], pre_dscore[...], TN)
        grad_packed[:, rows] = (full * scale).T.astype(bf16)

    for part, (left, right) in enumerate(((pre_dscore, packed), (pre_probs, cot))):
        whole = jnp.where(own_head, mm(left[...], right[:, :width]), 0.0)
        total = whole[:PAD]
        for h in range(1, heads):
            total = total + whole[h * PAD : (h + 1) * PAD]
        prefix_grad_ref[:, part * width : (part + 1) * width] = total

    for c in range(half):
        total = None
        for b in range(3):
            term = mm(grad_packed[:, b * width : (b + 1) * width], out_weight(b, c), NT)
            total = term if total is None else total + term
        acc_a[:, c * SLOT : (c + 1) * SLOT] = total

    @pl.loop(0, row_steps)
    def _(r):
        rows = pl.ds(r * rows_step, rows_step)
        acc_g[rows, :] += norm_backward(tok[rows, :].astype(f32), vec(0), acc_a[rows, :])

    in_copy = pltpu.make_async_copy(acc_g, input_grad_hbm, sem.at[3])
    in_copy.start()
    out_copy.wait()
    in_copy.wait()


def run_block(
    shards_count, prefix_count, tokens, cotangent, segments, vec, prefix_low, weights
):
    length, width = tokens.shape
    heads = width // HEAD_DIM
    hbm = pl.BlockSpec(memory_space=pl.ANY)
    vmem = pl.BlockSpec(memory_space=pltpu.VMEM)
    return pl.pallas_call(
        functools.partial(block_kernel, shards_count, prefix_count),
        out_shape=(
            jax.ShapeDtypeStruct((length, width), bf16),
            jax.ShapeDtypeStruct((length, width), f32),
            jax.ShapeDtypeStruct((PAD, 2 * width), f32),
        ),
        in_specs=[hbm, hbm, vmem, vmem, vmem, vmem, hbm],
        out_specs=(hbm, hbm, vmem),
        scratch_shapes=[
            pltpu.VMEM(weights.shape, bf16),
            pltpu.VMEM((length, width), bf16),
            pltpu.VMEM((length, width), bf16),
            pltpu.VMEM((length, width), bf16),
            pltpu.VMEM((length, 3 * width), bf16),
            pltpu.VMEM((width, length), bf16),
            pltpu.VMEM((width, length), bf16),
            pltpu.VMEM((heads, length, length), bf16),
            pltpu.VMEM((length, length), f32),
            pltpu.VMEM((heads * PAD, width), bf16),
            pltpu.VMEM((heads * PAD, width), bf16),
            pltpu.VMEM((heads * PAD, length), f32),
            pltpu.VMEM((heads * PAD, length), bf16),
            pltpu.VMEM((heads * PAD, length), bf16),
            pltpu.VMEM((width, length), f32),
            pltpu.VMEM((length, width), f32),
            pltpu.VMEM((length, width), f32),
            pltpu.VMEM((length, width), f32),
            pltpu.VMEM((length, width), bf16),
            pltpu.VMEM((length, 3 * width), bf16),
            pltpu.SemaphoreType.DMA((4,)),
            pltpu.SemaphoreType.DMA((12,)),
        ],
        compiler_params=pltpu.CompilerParams(vmem_limit_bytes=66_000_000),
    )(
        tokens,
        cotangent,
        segments[:, None],
        segments[None, :],
        vec,
        prefix_low,
        weights,
    )


def shards(
    tokens,
    segment_ids,
    cotangent,
    norm_in_gain,
    norm_in_shift,
    qkv_weight,
    qkv_bias,
    proj_weight,
    proj_bias,
    norm_mid_gain,
    norm_mid_shift,
    up_weight,
    up_bias,
    down_weight,
    down_bias,
    prefix_table,
    first_weight,
    first_bias,
    second_weight,
    second_bias,
):
    width = tokens.shape[-1]
    unit = qkv_weight.shape[0]
    count = width // unit
    reps = lax.axis_size("rep")
    prefix_count = prefix_table.shape[0]
    local = jnp.concatenate(
        [qkv_weight[:, b * width : (b + 1) * width] for b in range(3)]
        + [proj_weight]
        + [up_weight[:, b * width : (b + 1) * width] for b in range(4)]
        + [down_weight],
        axis=0,
    )
    share = local.shape[0] // reps
    mine = lax.dynamic_slice_in_dim(local, lax.axis_index("rep") * share, share, axis=0)
    weights = lax.all_gather(mine, ("dp", "rep"), axis=0, tiled=True).reshape(
        count, local.shape[0], width
    )
    small = jnp.concatenate(
        [
            part.reshape(-1, unit)
            for part in (
                norm_in_gain,
                norm_in_shift,
                proj_bias,
                norm_mid_gain,
                norm_mid_shift,
                down_bias,
            )
        ]
        + [qkv_bias.reshape(3, unit), up_bias.reshape(4, unit)],
        axis=0,
    )
    spread = lax.all_gather(small, "dp", axis=0)

    def line(i):
        return spread[:, i].reshape(1, width)

    vec = jnp.concatenate(
        [
            line(0),
            line(1),
            spread[:, 6:9].reshape(3, width),
            line(2),
            line(3),
            line(4),
            spread[:, 9:13].reshape(4, width),
            line(5),
            jnp.zeros((3, width), bf16),
        ],
        axis=0,
    ).astype(f32)
    hidden = jnp.tanh(
        jnp.dot(prefix_table, first_weight, preferred_element_type=f32) + first_bias.astype(f32)
    )
    hidden_low = hidden.astype(bf16)
    part = jnp.dot(hidden_low, second_weight, preferred_element_type=f32)
    part = lax.psum(part, "rep") + second_bias.astype(f32)
    prefix_kv = lax.all_gather(part, "dp", axis=1, tiled=True)
    prefix_low = jnp.pad(prefix_kv.astype(bf16), ((0, PAD - prefix_count), (0, 0)))
    activations, input_grad, prefix_grad = run_block(
        count,
        prefix_count,
        tokens[0],
        cotangent[0],
        segment_ids[0],
        vec,
        prefix_low,
        weights,
    )
    prefix_grad = prefix_grad[:prefix_count]
    owned = lax.psum(
        lax.psum_scatter(prefix_grad, "dp", scatter_dimension=1, tiled=True), "rep"
    )
    hidden_values = hidden_low.astype(f32)
    second_weight_grad = jnp.dot(
        hidden_values.T, owned, precision=highest, preferred_element_type=f32
    )
    second_bias_grad = jnp.sum(owned, axis=0)
    hidden_part = jnp.dot(
        owned, second_weight.astype(f32).T, precision=highest, preferred_element_type=f32
    )
    grad_hidden = lax.psum(hidden_part, "dp")
    grad_inner = grad_hidden * (1.0 - hidden * hidden)
    first_weight_grad = jnp.dot(
        prefix_table.astype(f32).T, grad_inner, precision=highest, preferred_element_type=f32
    )
    first_bias_grad = jnp.sum(grad_inner, axis=0)
    table_part = jnp.dot(
        grad_inner, first_weight.astype(f32).T, precision=highest, preferred_element_type=f32
    )
    prefix_table_grad = lax.psum(table_part, "rep")
    return (
        activations[None],
        input_grad[None],
        prefix_table_grad,
        first_weight_grad,
        first_bias_grad,
        second_weight_grad,
        second_bias_grad,
        prefix_kv,
    )


def solution(mesh):
    in_specs = (
        P(("dp", "rep"), None, None),
        P(("dp", "rep"), None),
        P(("dp", "rep"), None, None),
        P("dp"),
        P("dp"),
        P("dp", None),
        P("dp"),
        P("dp", None),
        P("dp"),
        P("dp"),
        P("dp"),
        P("dp", None),
        P("dp"),
        P("dp", None),
        P("dp"),
        P(),
        P(None, "rep"),
        P("rep"),
        P("rep", "dp"),
        P("dp"),
    )
    out_specs = (
        P(("dp", "rep"), None, None),
        P(("dp", "rep"), None, None),
        P(),
        P(None, "rep"),
        P("rep"),
        P("rep", "dp"),
        P("dp"),
        P(),
    )
    return jax.shard_map(shards, mesh=mesh, in_specs=in_specs, out_specs=out_specs, check_vma=False)
```

time: 669 us -> 396 us (0.59)
  matrix products: 121 us -> 3.18 us
  blocking collectives: 232 us -> 126 us
  Pallas kernels: 0 us -> 84.5 us
  waiting for transfers between devices: 228 us -> 147 us
  other arithmetic: 50.9 us -> 1.82 us
    all_gather x10 -> x2, blocking collectives: 172 us -> 50.6 us  [the longest x1 25.4 us: shards(): spread = lax.all_gather(small, 'dp', axis=0)]
    dot_general x24 -> x5, matrix products: 120 us -> 2.19 us  [the longest x1 1.42 us: shards(): jnp.dot(prefix_table.astype(f32).T, grad_inner, precision=highest, prefer...]
    all_gather x4 -> x1, waiting for transfers between devices: 194 us -> 89.7 us  [shards(): lax.all_gather(mine, ('dp', 'rep'), axis=0, tiled=True)]
    pallas_call x0 -> x1, Pallas kernels: none -> 84.5 us  [run_block(): pl.pallas_call(functools.partial(block_kernel, shards_count, prefix_count...]
    convert_element_type x13 -> x4, other arithmetic: 30.6 us -> 0.65 us  [the longest x1 0.64 us: shards(): vec = jnp.concatenate([line(0), line(1), spread[:, 6:9].reshape(3, width)...]
    reduce_scatter x1, waiting for transfers between devices: 31.6 us -> 57.2 us  [shards(): lax.psum_scatter(prefix_grad, 'dp', scatter_dimension=1, tiled=True)]
    psum x1 -> x2, blocking collectives: 12.3 us -> 28.8 us  [the longest x1 16.6 us: shards(): part = lax.psum(part, 'rep') + second_bias.astype(f32)]
    reduce_sum x7 -> x0, other arithmetic: 13.4 us -> none  [the longest x1 8.44 us: one_block(): jnp.sum(row_exp, axis=-1, keepdims=True)]
  transfers between devices with their start and end apart: 6 -> 2, of which waited for: 3 -> 2; matrix products, arithmetic and copies ran while one was open for 14% -> 1% of each run, Pallas kernels for 0% -> 0%
where the time goes in v1:
time: 396 us; the launch traced here: 395 us
  waiting for transfers between devices  147 us (37%)
  blocking collectives  126 us (32%)
  Pallas kernels  84.5 us (21%)
  local copies, waits for them, and re-layouts  17.4 us (4%)
  between operations  14.3 us (4%)
    all_gather x1, waiting for transfers between devices, shards(): lax.all_gather(mine, ('dp', 'rep'), axis=0, tiled=True)  89.7 us
    pallas_call x1, Pallas kernels, run_block(): pl.pallas_call(functools.partial(block_kernel, shards_count, prefix_count...  84.5 us
    reduce_scatter x1, waiting for transfers between devices, shards(): lax.psum_scatter(prefix_grad, 'dp', scatter_dimension=1, tiled=True)  57.2 us
    psum x1, blocking collectives, shards(): grad_hidden = lax.psum(hidden_part, 'dp')  28 us
    all_gather x1, blocking collectives, shards(): spread = lax.all_gather(small, 'dp', axis=0)  25.4 us
    all_gather x1, blocking collectives, shards(): prefix_kv = lax.all_gather(part, 'dp', axis=1, tiled=True)  25.2 us
    psum x1, blocking collectives, shards(): prefix_table_grad = lax.psum(table_part, 'rep')  19 us
    psum x1, blocking collectives, shards(): part = lax.psum(part, 'rep') + second_bias.astype(f32)  16.6 us
  transfers between devices with their start and end apart: 2, of which 2 were waited for; matrix products, arithmetic and copies ran while one was open for 1% of the time, Pallas kernels for 0%

profile of v1, /device:TPU:1, one launch (start us, length us, event | category | flops | bytes accessed | tf_op | source)
XLA Modules:
  0.0 394.7 jit_solution(3981492890228516249)
XLA Ops:
  7.3 1.8 slice_dynamic-update-slice_fusion.6
  9.1 1.7 slice_dynamic-update-slice_fusion.5
  10.7 1.7 slice_dynamic-update-slice_fusion.4
  12.4 1.7 constant_dynamic-update-slice_fusion.1
  14.0 1.7 slice_dynamic-update-slice_fusion.3
  15.8 1.7 slice_dynamic-update-slice_fusion.2
  17.6 0.7 slice_dynamic-update-slice_fusion.1
  18.3 0.7 slice_dynamic-update-slice_fusion
  19.0 1.1 constant_dynamic-update-slice_fusion
  20.1 2.1 constant_dynamic-slice_fusion
  22.3 0.1 concatenate.9
  22.4 25.4 %all-gather.1 = bf16[8,13,128]{2,1,0:T(8,128)(2,1)S(1)} all-gather(bf16[1,13,128]{2,1,0:T(8,128)(2,1)S(1)} %bitcast.42), channel_id=2, replica_groups=mesh['dp'=8,'rep'=4] {'dp'}, dimensions={0}, use_global_device_ids=true | all-gather | bytes 29952 | tf_op jit(solution)/shard_map/all_gather | solution.py:439
  48.1 0.6 convert_element_type.21.vec_ref
  48.7 0.2 fusion
  49.0 0.1 fusion.3
  49.1 16.6 %psum.28 = f32[10,256]{1,0:T(8,128)S(1)} all-reduce(f32[10,256]{1,0:T(8,128)S(1)} %fusion.3), channel_id=1, replica_groups=mesh['dp'=8,'rep'=4] {'rep'}, use_global_device_ids=true, to_apply=%region_0.0 | all-reduce | flops 2560 | bytes 20480 | tf_op jit(solution)/shard_map/psum | solution.py:463
  65.7 25.2 %all_gather.14 = f32[10,2048]{1,0:T(8,128)S(1)} all-gather(f32[10,256]{1,0:T(8,128)S(1)} %broadcast_add_fusion), channel_id=1, replica_groups=mesh['dp'=8,'rep'=4] {'dp'}, dimensions={1}, use_global_device_ids=true | all-gather | bytes 92160 | tf_op jit(solution)/shard_map/all_gather | solution.py:464
  90.9 0.6 pad.4.prefix_ref
  91.5 0.9 copy.31.seg_col
  92.4 89.7 %all-gather.4.cloned.1.call-done = bf16[12288,1024]{1,0:T(8,128)(2,1)} async-done(((bf16[384,1024]{1,0:T(8,128)(2,1)}), bf16[12288,1024]{1,0:T(8,128)(2,1)}) %all-gather.4.cloned.1.call-update) | async-done | bytes 25165840 | tf_op jit(solution)/shard_map/all_gather | solution.py:421
  182.1 84.5 %shard_map.251 = (bf16[512,1024]{1,0:T(8,128)(2,1)}, f32[512,1024]{1,0:T(8,128)}, f32[16,2048]{1,0:T(8,128)}) custom-call(bf16[512,1024]{1,0:T(8,128)(2,1)} %bitcast.39, bf16[512,1024]{1,0:T(8,128)(2,1)} %bitcast.40, s32[512,1]{1,0:T(8,128)} %copy.31.seg_col, s32[1,512]{1,0:T(1,128)} %seg_row.1, f32[16,1024]{1,0:T(8,128)} %convert_element_type.21.vec_ref, ...), custom_call_target="tpu_custom_call" | custom-call | tf_op jit(solution)/shard_map/pallas_call | solution.py:340
  266.7 57.2 %reduce-scatter.2.cloned.1.call-done = f32[10,256]{1,0:T(8,128)} async-done(((f32[10,2048]{1,0:T(8,128)}), f32[10,256]{1,0:T(8,128)}) %reduce-scatter.2.cloned.1.call-update) | async-done | bytes 10256 | tf_op jit(solution)/shard_map/reduce_scatter | solution.py:478
  323.9 12.3 %psum.29 = f32[10,256]{1,0:T(8,128)S(1)} all-reduce(f32[10,256]{1,0:T(8,128)} %reduce-scatter.2.cloned.1.call-done), channel_id=1, replica_groups=mesh['dp'=8,'rep'=4] {'rep'}, use_global_device_ids=true, to_apply=%region_2.3 | all-reduce | flops 2560 | bytes 20480 | tf_op jit(solution)/shard_map/psum | solution.py:477
  336.2 0.1 fusion.7
  336.3 28.0 %psum.30 = f32[10,200]{1,0:T(8,128)S(1)} all-reduce(f32[10,200]{1,0:T(8,128)S(1)} %fusion.7), channel_id=1, replica_groups=mesh['dp'=8,'rep'=4] {'dp'}, use_global_device_ids=true, to_apply=%region_3.4 | all-reduce | flops 2000 | bytes 16000 | tf_op jit(solution)/shard_map/psum | solution.py:488
  364.3 0.6 fusion.5
  364.9 0.3 fusion.6
  365.2 1.0 fusion.1
  366.2 1.4 convolution_bitcast_fusion
  367.6 0.6 reduce_sum.19
  368.2 19.0 %psum.31 = f32[10,1024]{1,0:T(8,128)} all-reduce(f32[10,1024]{1,0:T(8,128)S(1)} %fusion.6), channel_id=1, replica_groups=mesh['dp'=8,'rep'=4] {'rep'}, use_global_device_ids=true, to_apply=%region_4.5 | all-reduce | flops 10240 | bytes 81920 | tf_op jit(solution)/shard_map/psum | solution.py:497
  387.2 0.7 copy.41
  (47 shorter events, 0.4 us)
Async XLA Ops:
  7.2 41.6 %copy-start = (bf16[1024,200]{0,1:T(8,128)(2,1)S(1)}, bf16[1024,200]{0,1:T(8,128)(2,1)}, u32[]{:S(2)}) copy-start(bf16[1024,200]{0,1:T(8,128)(2,1)} %param.36) | copy-start | bytes 1228804
  7.2 10.4 %copy-start.1 = (bf16[128,4096]{1,0:T(8,128)(2,1)S(1)}, bf16[128,4096]{1,0:T(8,128)(2,1)}, u32[]{:S(2)}) copy-start(bf16[128,4096]{1,0:T(8,128)(2,1)} %param.31) | copy-start | bytes 3145732
  7.2 11.8 %copy-start.2 = (bf16[512,1024]{1,0:T(8,128)(2,1)S(1)}, bf16[512,1024]{1,0:T(8,128)(2,1)}, u32[]{:S(2)}) copy-start(bf16[512,1024]{1,0:T(8,128)(2,1)} %param.33) | copy-start | bytes 3145732
  7.2 174.9 %all-gather.4.cloned.1.call-start = ((), (), s32[]{:S(2)}) async-start(), calls=%async_computation.1 | async-start | bytes 25952256 | tf_op jit(solution)/shard_map/all_gather | solution.py:421
  15.7 6.5 %copy-start.6 = (bf16[384]{0:T(512)(128)(2,1)S(1)}, bf16[384]{0:T(512)(128)(2,1)}, u32[]{:S(2)}) copy-start(bf16[384]{0:T(512)(128)(2,1)} %param.26) | copy-start | bytes 2308
  15.7 6.5 %copy-start.7 = (bf16[512]{0:T(512)(128)(2,1)S(1)}, bf16[512]{0:T(512)(128)(2,1)}, u32[]{:S(2)}) copy-start(bf16[512]{0:T(512)(128)(2,1)} %param.32) | copy-start | bytes 3076
  15.7 6.5 %copy-start.8 = (bf16[128]{0:T(256)(128)(2,1)S(1)}, bf16[128]{0:T(256)(128)(2,1)}, u32[]{:S(2)}) copy-start(bf16[128]{0:T(256)(128)(2,1)} %param.23) | copy-start | bytes 772
  15.7 6.5 %copy-start.9 = (bf16[128]{0:T(256)(128)(2,1)S(1)}, bf16[128]{0:T(256)(128)(2,1)}, u32[]{:S(2)}) copy-start(bf16[128]{0:T(256)(128)(2,1)} %param.24) | copy-start | bytes 772
  15.7 6.5 %copy-start.10 = (bf16[128]{0:T(256)(128)(2,1)S(1)}, bf16[128]{0:T(256)(128)(2,1)}, u32[]{:S(2)}) copy-start(bf16[128]{0:T(256)(128)(2,1)} %param.28) | copy-start | bytes 772
  15.7 6.5 %copy-start.11 = (bf16[128]{0:T(256)(128)(2,1)S(1)}, bf16[128]{0:T(256)(128)(2,1)}, u32[]{:S(2)}) copy-start(bf16[128]{0:T(256)(128)(2,1)} %param.29) | copy-start | bytes 772
  15.7 6.5 %copy-start.12 = (bf16[128]{0:T(256)(128)(2,1)S(1)}, bf16[128]{0:T(256)(128)(2,1)}, u32[]{:S(2)}) copy-start(bf16[128]{0:T(256)(128)(2,1)} %param.30) | copy-start | bytes 772
  15.8 6.5 %copy-start.13 = (bf16[128]{0:T(256)(128)(2,1)S(1)}, bf16[128]{0:T(256)(128)(2,1)}, u32[]{:S(2)}) copy-start(bf16[128]{0:T(256)(128)(2,1)} %param.34) | copy-start | bytes 772
  15.8 32.1 %copy-start.14 = (bf16[200]{0:T(256)(128)(2,1)S(1)}, bf16[200]{0:T(256)(128)(2,1)}, u32[]{:S(2)}) copy-start(bf16[200]{0:T(256)(128)(2,1)} %param.37) | copy-start | bytes 1204
  15.8 32.1 %copy-start.15 = (bf16[256]{0:T(256)(128)(2,1)S(1)}, bf16[256]{0:T(256)(128)(2,1)}, u32[]{:S(2)}) copy-start(bf16[256]{0:T(256)(128)(2,1)} %param.39) | copy-start | bytes 1540
  15.8 32.9 %copy-start.4 = (bf16[10,1024]{1,0:T(8,128)(2,1)S(1)}, bf16[10,1024]{1,0:T(8,128)(2,1)}, u32[]{:S(2)}) copy-start(bf16[10,1024]{1,0:T(8,128)(2,1)} %param.35) | copy-start | bytes 61444
  17.6 31.4 %copy-start.3 = (bf16[200,256]{1,0:T(8,128)(2,1)S(1)}, bf16[200,256]{1,0:T(8,128)(2,1)}, u32[]{:S(2)}) copy-start(bf16[200,256]{1,0:T(8,128)(2,1)} %param.38) | copy-start | bytes 307204
  18.3 73.2 %copy-start.5 = (s32[1,512]{1,0:T(1,128)S(1)}, s32[1,512]{1,0:T(1,128)}, u32[]{:S(2)}) copy-start(s32[1,512]{1,0:T(1,128)} %seg_row.1) | copy-start | bytes 6148
  22.2 301.7 %reduce-scatter.2.cloned.1.call-start = ((), (), s32[]{:S(2)}) async-start(), calls=%async_computation.2 | async-start | bytes 147456 | tf_op jit(solution)/shard_map/reduce_scatter | solution.py:478
Sparse Core Ops, SparseCore 0:
  22.3 159.7 all-gather.3
  266.8 57.0 reduce-scatter.1

commit v2 on v1

v2 whole, which is shorter than its diff:
```python
import functools

import jax
import jax.numpy as jnp
from jax import lax
from jax.experimental import pallas as pl
from jax.experimental.pallas import tpu as pltpu
from jax.sharding import PartitionSpec as P

HEAD_DIM = 64
PAIR = 2 * HEAD_DIM
CHUNK = 512
PAD = 16
ROWS = 128
SLOTS = 12
PARTS = 4
LEAD = 2
MESH = pl.DeviceIdType.MESH
VEC_ROWS = ((0, 1), (1, 1), (2, 3), (5, 1), (6, 1), (7, 1), (8, 4), (12, 1))

eps_norm = 1e-05
neg_fill = -1e30
highest = lax.Precision.HIGHEST
f32 = jnp.float32
bf16 = jnp.bfloat16

NN = (((1,), (0,)), ((), ()))
NT = (((1,), (1,)), ((), ()))
TN = (((0,), (0,)), ((), ()))


def mm(left, right, dims=NN):
    return lax.dot_general(left, right, dims, preferred_element_type=f32)


def normalise(values):
    centred = values - jnp.mean(values, axis=-1, keepdims=True)
    variance = jnp.mean(centred * centred, axis=-1, keepdims=True)
    inverse = lax.rsqrt(variance + eps_norm)
    return centred * inverse, inverse


def norm_backward(values, gain, upstream):
    unit, inverse = normalise(values)
    scaled = upstream * gain
    return inverse * (
        scaled
        - jnp.mean(scaled, axis=-1, keepdims=True)
        - unit * jnp.mean(scaled * unit, axis=-1, keepdims=True)
    )


def neighbours(dp, rep):
    return (dp + 1 - 2 * (dp % 2), rep), (dp, rep + 2 - 4 * (rep // 2)), (dp, rep + 1 - 2 * (rep % 2))


def remote(src, dst, send_sem, recv_sem, device):
    return pltpu.make_async_remote_copy(
        src_ref=src,
        dst_ref=dst,
        send_sem=send_sem,
        recv_sem=recv_sem,
        device_id=device,
        device_id_type=MESH,
    )


def pick(z, values):
    out = jnp.int32(values[-1])
    for i in range(len(values) - 2, -1, -1):
        out = jnp.where(z == i, values[i], out)
    return out


def gather_steps(weights, own_sem, sib_sem, z_sem, y_sem, x_sem, send_sem, zsend_sem):
    dp = lax.axis_index("dp")
    rep = lax.axis_index("rep")
    z = dp // 2
    x = dp % 2
    y = rep // 2
    core = rep % 2
    cols = weights.shape[2] // 2
    planes = [pick(z, v) for v in ((1, 0, 1, 2), (2, 2, 3, 1), (3, 3, 0, 0))]
    hops = [pick(z, v) for v in ((1, 1, 1, 1), (2, 1, 1, 2), (3, 2, 2, 3))]
    x_dev, y_dev, core_dev = neighbours(dp, rep)
    up = (dp + 2, rep)
    down = (dp - 2, rep)
    x_shard = dp + 1 - 2 * x

    def region(slot, shard, count, row, rows):
        return weights.at[
            pl.ds(shard, count),
            pl.ds(pl.multiple_of(slot * ROWS + row, 16), rows),
            pl.ds(pl.multiple_of(core * cols, 128), cols),
        ]

    def move(part, send, recv, device):
        return remote(part, part, send, recv, device)

    z_row = 16 * (4 * y + x)
    y_row = 16 * (4 * (1 - y) + x)
    x_row = 16 * (4 * y + 3 * x)
    far_row = 16 * (4 * (1 - y) + 3 * x)

    def guarded(slot, f):
        pl.when((slot >= 0) & (slot < SLOTS))(functools.partial(f, slot))

    def send_own(s):
        move(region(s, dp, 1, 0, ROWS), send_sem.at[s], own_sem.at[s], x_dev).start()

    def take_own(s):
        part = region(s, x_shard, 1, 0, ROWS)
        move(part, send_sem.at[s], own_sem.at[s], x_dev).wait_recv()
        plane = region(s, 2 * z, 2, z_row, 48)

        @pl.when(z < 3)
        def _():
            move(plane, zsend_sem.at[s, 0], z_sem.at[s, z], up).start()

        @pl.when(z > 0)
        def _():
            move(plane, zsend_sem.at[s, 1], z_sem.at[s, z], down).start()

        move(part, send_sem.at[s], sib_sem.at[s], core_dev).start()

    def take_z(i, s):
        p = planes[i]
        part = region(s, 2 * p, 2, z_row, 48)
        move(part, zsend_sem.at[s, 2 + i], z_sem.at[s, p], x_dev).wait_recv()

        @pl.when((p < z) & (z < 3))
        def _():
            move(part, zsend_sem.at[s, 2 + i], z_sem.at[s, p], up).start()

        @pl.when((p > z) & (z > 0))
        def _():
            move(part, zsend_sem.at[s, 2 + i], z_sem.at[s, p], down).start()

        move(part, send_sem.at[s], y_sem.at[s, p], y_dev).start()
        move(region(s, 2 * p, 2, x_row, 16), send_sem.at[s], x_sem.at[s, p], x_dev).start()

    def take_y(i, s):
        p = planes[i]
        move(region(s, 2 * p, 2, y_row, 48), send_sem.at[s], y_sem.at[s, p], y_dev).wait_recv()
        move(region(s, 2 * p, 2, far_row, 16), send_sem.at[s], x_sem.at[s, p], x_dev).start()

    def take_x(i, s):
        p = planes[i]
        move(region(s, 2 * p, 2, 0, 32), send_sem.at[s], x_sem.at[s, p], x_dev).wait_recv()
        move(region(s, 2 * p, 2, 0, ROWS), send_sem.at[s], sib_sem.at[s], core_dev).start()

    def take_core(s):
        move(region(s, 0, 7, 0, ROWS), send_sem.at[s], sib_sem.at[s], core_dev).wait_recv()

    def step(u):
        t = u // PARTS
        part = u % PARTS

        @pl.when(part == 0)
        def _():
            guarded(t, send_own)
            guarded(t - LEAD, take_own)
            guarded(t - LEAD - hops[0], functools.partial(take_z, 0))

        @pl.when(part == 1)
        def _():
            guarded(t - LEAD - hops[1], functools.partial(take_z, 1))
            guarded(t - LEAD - hops[2], functools.partial(take_z, 2))

        @pl.when(part == 2)
        def _():
            for i in range(3):
                guarded(t - LEAD - 1 - hops[i], functools.partial(take_y, i))

        @pl.when(part == 3)
        def _():
            for i in range(3):
                guarded(t - LEAD - 2 - hops[i], functools.partial(take_x, i))
            guarded(t - LEAD - 6, take_core)

    def finish():
        @pl.loop(0, SLOTS)
        def _(s):
            sent = weights.at[pl.ds(0, 4), pl.ds(0, 752), pl.ds(0, cols // 2)]
            move(sent, send_sem.at[s], own_sem.at[s], x_dev).wait_send()
            plane = region(s, 0, 2, 0, 48)

            def done(i):
                move(plane, zsend_sem.at[s, i], z_sem.at[s, z], x_dev).wait_send()

            pl.when(z < 3)(functools.partial(done, 0))
            pl.when(z > 0)(functools.partial(done, 1))
            for i in range(3):
                p = planes[i]
                pl.when(((p < z) & (z < 3)) | ((p > z) & (z > 0)))(functools.partial(done, 2 + i))

    return step, finish


def exchange(ref, own, sems, axis, count):
    dp = lax.axis_index("dp")
    rep = lax.axis_index("rep")

    def start(source=None):
        for i in range(1, count):
            if axis == "dp":
                device = (lax.rem(dp + i, count), rep)
                slot = lax.rem(dp + i, count)
            else:
                device = (dp, lax.rem(rep + i, count))
                slot = lax.rem(rep + i, count)
            src = ref.at[own] if source is None else source.at[slot]
            remote(src, ref.at[own], sems.at[0], sems.at[1], device).start()

    def wait():
        rest = ref.at[pl.ds(0, count - 1)]
        both = remote(rest, rest, sems.at[0], sems.at[1], (dp, lax.rem(rep + 1, 4)))
        both.wait_recv()
        both.wait_send()

    return start, wait


def block_kernel(comm, count, prefix_count, *refs):
    refs = list(refs)

    def take(number):
        out = refs[:number]
        del refs[:number]
        return out

    tokens_hbm, cotangent_hbm, seg_row = take(3)
    if comm:
        (small, table, first_w, first_b, second_w, second_b) = take(6)
        (qkv_hbm, proj_hbm, up_hbm, down_hbm) = take(4)
        (
            activations_hbm,
            input_grad_hbm,
            table_grad,
            first_w_grad,
            first_b_grad,
            second_w_grad,
            second_b_grad,
            prefix_kv,
        ) = take(8)
    else:
        small, prefix_in, weights_hbm = take(3)
        activations_hbm, input_grad_hbm, prefix_grad_out = take(3)
    (
        weights,
        tok,
        cot,
        normed,
        packed,
        keys_t,
        values_t,
        probs,
        bias_t,
        key_pre,
        value_pre,
        pre_f32,
        pre_probs,
        pre_dscore,
        mixed_t,
        acc_a,
        acc_g,
        resid,
        attended,
        grad_packed,
        vec_ref,
        sem,
        wsem,
    ) = take(23)
    if comm:
        (small_all, part_all, kv_all, grad_blocks, red_dp, red_rep, red_hidden, red_table) = take(8)
        (small_sem, part_sem, kv_sem, red_sem) = take(4)
        gather_sems = take(7)

    length, width = tok.shape
    heads = width // HEAD_DIM
    unit = width // count
    half = width // CHUNK
    scale = HEAD_DIM ** (-0.5)
    group = count // half
    zero = jnp.zeros((), bf16)

    copies = [
        pltpu.make_async_copy(tokens_hbm, tok, sem.at[0]),
        pltpu.make_async_copy(cotangent_hbm, cot, sem.at[1]),
    ]
    if comm:
        dp = lax.axis_index("dp")
        rep = lax.axis_index("rep")
        pieces = [qkv_hbm.at[:, b * width : (b + 1) * width] for b in range(3)] + [proj_hbm]
        pieces += [down_hbm]
        pieces += [up_hbm.at[:, b * width : (b + 1) * width] for b in range(4)]
        row = 0
        loads = []
        for i, piece in enumerate(pieces):
            rows = 4 * unit if i == 4 else unit
            loads.append(
                pltpu.make_async_copy(piece, weights.at[dp, pl.ds(row, rows), :], wsem.at[i])
            )
            row += rows
        for c in loads[:4] + copies + loads[4:]:
            c.start()
        barrier = pltpu.get_barrier_semaphore()
        for i in range(1, 8):
            pl.semaphore_signal(
                barrier, inc=1, device_id=(lax.rem(dp + i, 8), rep), device_id_type=MESH
            )
        for i in range(1, 4):
            pl.semaphore_signal(
                barrier, inc=1, device_id=(dp, lax.rem(rep + i, 4)), device_id_type=MESH
            )
        small_all[dp] = small[...]
        hidden = jnp.tanh(mm(table[...], first_w[...]) + first_b[...].astype(f32))
        hidden_low = hidden.astype(bf16)
        part_all[rep] = jnp.zeros(part_all.shape[1:], f32)
        part_all[rep, :prefix_count, :] = mm(hidden_low, second_w[...])
        for c in loads:
            c.wait()
        pl.semaphore_wait(barrier, 10)
        step, finish_gather = gather_steps(weights, *gather_sems)
        small_start, small_wait = exchange(small_all, dp, small_sem, "dp", 8)
        part_start, part_wait = exchange(part_all, rep, part_sem, "rep", 4)
        kv_start, kv_wait = exchange(kv_all, dp, kv_sem, "dp", 8)
        step(0)
        small_start()
        part_start()
        now = [1]

        def run(number):
            if number > 0:
                first = now[0]
                now[0] += number
                pl.loop(first, first + number)(step)

        def until(slot):
            run(PARTS * (slot + LEAD + 7) - now[0])

    else:
        loads = [
            pltpu.make_async_copy(
                weights_hbm.at[:, pl.ds(b * unit, unit), :],
                weights.at[:, pl.ds(b * unit, unit), :],
                wsem.at[b],
            )
            for b in range(12)
        ]
        for c in copies + loads:
            c.start()
        for c in loads:
            c.wait()

    def in_weight(block, col):
        return weights[:, pl.ds(block * unit, unit), pl.ds(col, CHUNK)].reshape(width, CHUNK)

    def out_weight(block, c):
        return weights[pl.ds(c * group, group), pl.ds(block * unit, unit), :].reshape(CHUNK, width)

    def vec(row, col=0, size=None):
        return vec_ref[pl.ds(row, 1), pl.ds(col, width if size is None else size)]

    rows_step = 128
    row_steps = length // rows_step

    seg_col = jnp.broadcast_to(seg_row[...].astype(f32), (rows_step, length)).T
    attended[...] = jnp.concatenate([seg_col] * (width // rows_step), axis=1).astype(bf16)

    @pl.loop(0, row_steps)
    def _(r):
        rows = pl.ds(r * rows_step, rows_step)
        key_pos = lax.broadcasted_iota(jnp.int32, (rows_step, length), 0) + r * rows_step
        query_pos = lax.broadcasted_iota(jnp.int32, (rows_step, length), 1)
        same = attended[rows, :length].astype(f32) == seg_row[...].astype(f32)
        bias_t[rows, :] = jnp.where(same & (key_pos <= query_pos), 0.0, neg_fill)

    if comm:
        run(3)
        small_wait()
        for j in range(count):
            part = small_all[j].astype(f32)
            row = 0
            for first, number in VEC_ROWS:
                for r in range(number):
                    at = (j * number + r) * unit
                    col = at % width
                    vec_ref[first + at // width : first + at // width + 1, col : col + unit] = part[
                        row : row + 1
                    ]
                    row += 1
    else:
        vec_ref[...] = small[...]

    copies[0].wait()
    if comm:
        first_norm = now[0]
        now[0] += row_steps

    @pl.loop(0, row_steps)
    def _(r):
        rows = pl.ds(r * rows_step, rows_step)
        unit_rows, _ = normalise(tok[rows, :].astype(f32))
        normed[rows, :] = (unit_rows * vec(0) + vec(1)).astype(bf16)
        if comm:
            step(first_norm + r)

    if comm:
        part_wait()
        total = part_all[0] + part_all[1] + part_all[2] + part_all[3]
        kv_all[dp] = total + second_b[...].astype(f32)
        run(4)
        kv_start()

    def project(s):
        block = s // half
        col = (s % half) * CHUNK
        out = mm(normed[...], in_weight(block, col)) + vec(2 + block, col, CHUNK)
        factor = jnp.where(block == 0, scale, 1.0).astype(bf16)
        packed[:, pl.ds(s * CHUNK, CHUNK)] = out.astype(bf16) * factor

    if comm:
        until(0)
        first_qkv = now[0]
        now[0] += 3 * PARTS

        @pl.loop(0, 3 * half)
        def _(s):
            project(s)
            for k in range(PARTS // half):
                step(first_qkv + s * (PARTS // half) + k)
    else:
        pl.loop(0, 3 * half)(project)

    head_of_row = lax.broadcasted_iota(jnp.int32, (heads * PAD, width), 0) // PAD
    head_of_col = lax.broadcasted_iota(jnp.int32, (heads * PAD, width), 1) // HEAD_DIM
    own_head = head_of_row == head_of_col
    if comm:
        kv_wait()
        whole_kv = jnp.concatenate([kv_all[j] for j in range(count)], axis=1)
        prefix_kv[...] = whole_kv[:prefix_count]
        prefix_low = whole_kv.astype(bf16)
    else:
        prefix_low = prefix_in[...]
    key_pre[...] = jnp.where(own_head, jnp.concatenate([prefix_low[:, :width]] * heads, axis=0), zero)
    value_pre[...] = jnp.where(
        own_head, jnp.concatenate([prefix_low[:, width:]] * heads, axis=0), zero
    )
    pre_scores = mm(key_pre[...], packed[:, :width], NT)
    pad_row = lax.broadcasted_iota(jnp.int32, pre_scores.shape, 0) % PAD
    pre_f32[...] = jnp.where(pad_row < prefix_count, pre_scores, neg_fill)

    q_blocks = ((0, length // 2, length // 2), (length // 2, length // 2, length))
    lane_head = lax.broadcasted_iota(jnp.int32, (length, PAIR), 1) // HEAD_DIM

    if comm:
        first_attend = now[0]
        now[0] += heads // 2

    @pl.loop(0, heads // 2)
    def _(p):
        col = pl.multiple_of(p * PAIR, PAIR)
        q_pair = packed[:, pl.ds(col, PAIR)]
        k_pair = packed[:, pl.ds(width + col, PAIR)]
        v_pair = packed[:, pl.ds(2 * width + col, PAIR)]
        keys_t[pl.ds(col, PAIR), :] = k_pair.T
        values_t[pl.ds(col, PAIR), :] = v_pair.T
        for e in range(2):
            k_head = jnp.where(lane_head == e, k_pair, zero)
            head = 2 * p + e
            feat = pl.ds(pl.multiple_of(head * HEAD_DIM, HEAD_DIM), HEAD_DIM)
            pre_rows = pl.ds(pl.multiple_of(head * PAD, PAD), PAD)
            for q0, q_size, k_size in q_blocks:
                s = mm(k_head[:k_size], q_pair[q0 : q0 + q_size], NT)
                s = s + bias_t[:k_size, q0 : q0 + q_size]
                sp = pre_f32[pre_rows, q0 : q0 + q_size]
                top = jnp.maximum(
                    jnp.max(s, axis=0, keepdims=True), jnp.max(sp, axis=0, keepdims=True)
                )
                s = jnp.exp(s - top)
                sp = jnp.exp(sp - top)
                inverse = 1.0 / (
                    jnp.sum(s, axis=0, keepdims=True) + jnp.sum(sp, axis=0, keepdims=True)
                )
                own = (s * inverse).astype(bf16)
                probs[head, :k_size, q0 : q0 + q_size] = own
                pre_probs[pre_rows, q0 : q0 + q_size] = (sp * inverse).astype(bf16)
                mixed_t[feat, q0 : q0 + q_size] = mm(values_t[feat, :k_size], own)
        if comm:
            step(first_attend + p)

    if comm:
        first_turn = now[0]
        now[0] += width // 128

    @pl.loop(0, width // 128)
    def _(i):
        rows = pl.ds(pl.multiple_of(i * 128, 128), 128)
        full = mixed_t[rows, :] + mm(value_pre[:, rows], pre_probs[...], TN)
        attended[:, rows] = full.T.astype(bf16)
        if comm:
            step(first_turn + i)

    @pl.loop(0, half)
    def _(c):
        cols = pl.ds(pl.multiple_of(c * CHUNK, CHUNK), CHUNK)
        out = mm(attended[...], in_weight(3, c * CHUNK)) + vec(5, c * CHUNK, CHUNK)
        resid[:, cols] = tok[:, cols].astype(f32) + out

    if comm:
        first_mid = now[0]
        now[0] += row_steps

    @pl.loop(0, row_steps)
    def _(r):
        rows = pl.ds(r * rows_step, rows_step)
        unit_rows, _ = normalise(resid[rows, :])
        normed[rows, :] = (unit_rows * vec(6) + vec(7)).astype(bf16)
        if comm:
            step(first_mid + r)

    copies[1].wait()

    ff_steps = 4 * half
    root = 0.7978845608028654
    cube = 0.044715

    def feed(i, mid_step=lambda k: None):
        col = (i % half) * CHUNK
        w_up = in_weight(8 + i // half, col)
        w_down = weights[
            pl.ds(i * (count // ff_steps), count // ff_steps), pl.ds(4 * unit, 4 * unit), :
        ].reshape(CHUNK, width)
        pre = mm(normed[...], w_up) + vec(8 + i // half, col, CHUNK)
        square = pre * pre
        t = jnp.tanh(root * (pre + cube * (square * pre)))
        act = (0.5 * pre * (1.0 + t)).astype(bf16)
        slope = 0.5 * (1.0 + t) + (0.5 * root) * pre * (1.0 - t * t) * (
            1.0 + (3.0 * cube) * square
        )
        grad_act = mm(cot[...], w_down, NT)
        grad_pre = (grad_act * slope).astype(bf16)
        mid_step(0)
        acc_a[...] = jnp.where(i == 0, 0.0, acc_a[...]) + mm(act, w_down)
        mid_step(1)
        acc_g[...] = jnp.where(i == 0, 0.0, acc_g[...]) + mm(grad_pre, w_up, NT)

    if comm:
        until(8)
        first_feed = now[0]
        now[0] += 3 * PARTS

        @pl.loop(0, 6)
        def _(i):
            feed(i, lambda k: step(first_feed + 2 * i + k))

        pl.loop(6, ff_steps)(feed)
    else:
        pl.loop(0, ff_steps)(feed)

    @pl.loop(0, row_steps)
    def _(r):
        rows = pl.ds(r * rows_step, rows_step)
        attended[rows, :] = (resid[rows, :] + acc_a[rows, :] + vec(12)).astype(bf16)
        grad = cot[rows, :].astype(f32) + norm_backward(resid[rows, :], vec(6), acc_g[rows, :])
        acc_g[rows, :] = grad
        normed[rows, :] = grad.astype(bf16)

    out_copy = pltpu.make_async_copy(attended, activations_hbm, sem.at[2])
    out_copy.start()
    for c in range(half):
        cot[:, c * CHUNK : (c + 1) * CHUNK] = mm(normed[...], out_weight(3, c), NT).astype(bf16)
    pre_f32[...] = mm(value_pre[...], cot[...], NT)

    @pl.loop(0, heads // 2)
    def _(p):
        col = pl.multiple_of(p * PAIR, PAIR)
        q_pair = packed[:, pl.ds(col, PAIR)]
        v_pair = packed[:, pl.ds(2 * width + col, PAIR)]
        g_pair = cot[:, pl.ds(col, PAIR)]
        key_grad = jnp.zeros((length, PAIR), f32)
        value_grad = jnp.zeros((length, PAIR), f32)
        for e in range(2):
            own_lanes = lane_head == e
            v_head = jnp.where(own_lanes, v_pair, zero)
            q_head = jnp.where(own_lanes, q_pair, zero)
            g_head = jnp.where(own_lanes, g_pair, zero)
            head = 2 * p + e
            feat = pl.ds(pl.multiple_of(head * HEAD_DIM, HEAD_DIM), HEAD_DIM)
            pre_rows = pl.ds(pl.multiple_of(head * PAD, PAD), PAD)
            for q0, q_size, k_size in q_blocks:
                dp_own = mm(v_head[:k_size], g_pair[q0 : q0 + q_size], NT)
                own_low = probs[head, :k_size, q0 : q0 + q_size]
                own = own_low.astype(f32)
                pre = pre_probs[pre_rows, q0 : q0 + q_size].astype(f32)
                pre_dp = pre_f32[pre_rows, q0 : q0 + q_size]
                dot = jnp.sum(own * dp_own, axis=0, keepdims=True) + jnp.sum(
                    pre * pre_dp, axis=0, keepdims=True
                )
                ds = (own * (dp_own - dot)).astype(bf16)
                pre_dscore[pre_rows, q0 : q0 + q_size] = (pre * (pre_dp - dot)).astype(bf16)
                mixed_t[feat, q0 : q0 + q_size] = mm(keys_t[feat, :k_size], ds)
                dk = mm(ds, q_head[q0 : q0 + q_size])
                dv = mm(own_low, g_head[q0 : q0 + q_size])
                if k_size < length:
                    fill = jnp.zeros((length - k_size, PAIR), f32)
                    dk = jnp.concatenate([dk, fill], axis=0)
                    dv = jnp.concatenate([dv, fill], axis=0)
                key_grad = key_grad + dk
                value_grad = value_grad + dv
        grad_packed[:, pl.ds(width + col, PAIR)] = key_grad.astype(bf16)
        grad_packed[:, pl.ds(2 * width + col, PAIR)] = value_grad.astype(bf16)

    sums = []
    for left, right in ((pre_dscore, packed), (pre_probs, cot)):
        whole = jnp.where(own_head, mm(left[...], right[:, :width]), 0.0)
        total = whole[:PAD]
        for h in range(1, heads):
            total = total + whole[h * PAD : (h + 1) * PAD]
        sums.append(total)
    prefix_grad = jnp.concatenate(sums, axis=1)
    if comm:
        wide = 2 * unit
        for j in range(count):
            grad_blocks[j] = prefix_grad[:, j * wide : (j + 1) * wide]
        red_dp[dp] = grad_blocks[dp]
    else:
        prefix_grad_out[...] = prefix_grad

    @pl.loop(0, width // 128)
    def _(i):
        rows = pl.ds(pl.multiple_of(i * 128, 128), 128)
        full = mixed_t[rows, :] + mm(key_pre[:, rows], pre_dscore[...], TN)
        grad_packed[:, rows] = (full * scale).T.astype(bf16)

    def back_project(c):
        total = None
        for b in range(3):
            term = mm(grad_packed[:, b * width : (b + 1) * width], out_weight(b, c), NT)
            total = term if total is None else total + term
        acc_a[:, c * CHUNK : (c + 1) * CHUNK] = total

    def back_norm(r):
        rows = pl.ds(r * rows_step, rows_step)
        acc_g[rows, :] += norm_backward(tok[rows, :].astype(f32), vec(0), acc_a[rows, :])

    if comm:
        dp_start, dp_wait = exchange(red_dp, dp, red_sem.at[0], "dp", 8)
        rep_start, rep_wait = exchange(red_rep, rep, red_sem.at[1], "rep", 4)
        hid_start, hid_wait = exchange(red_hidden, dp, red_sem.at[2], "dp", 8)
        tab_start, tab_wait = exchange(red_table, rep, red_sem.at[3], "rep", 4)

        def tree(ref, number):
            total = ref[0]
            for j in range(1, number):
                total = total + ref[j]
            return total

        def exact(left, right, dims):
            return lax.dot_general(
                left, right, dims, precision=highest, preferred_element_type=f32
            )

        dp_start(grad_blocks)
        back_project(0)
        dp_wait()
        red_rep[rep] = tree(red_dp, 8)
        rep_start()
        back_project(1)
        rep_wait()
        owned = tree(red_rep, 4)
        red_hidden[dp] = exact(owned, second_w[...].astype(f32), NT)
        pl.loop(0, 1)(back_norm)
        hid_start()
        owned_rows = owned[:prefix_count]
        hidden_again = jnp.tanh(mm(table[...], first_w[...]) + first_b[...].astype(f32))
        second_w_grad[...] = exact(hidden_again.astype(bf16).astype(f32), owned_rows, TN)
        second_b_grad[...] = jnp.sum(owned, axis=0, keepdims=True)
        pl.loop(1, 2)(back_norm)
        hid_wait()
        inner = tree(red_hidden, 8)[:prefix_count] * (1.0 - hidden_again * hidden_again)
        red_table[rep, :prefix_count, :] = exact(inner, first_w[...].astype(f32), NT)
        first_w_grad[...] = exact(table[...].astype(f32), inner, TN)
        first_b_grad[...] = jnp.sum(inner, axis=0, keepdims=True)
        tab_start()
        pl.loop(2, row_steps)(back_norm)
    else:
        for c in range(half):
            back_project(c)
        pl.loop(0, row_steps)(back_norm)

    in_copy = pltpu.make_async_copy(acc_g, input_grad_hbm, sem.at[3])
    in_copy.start()
    if comm:
        tab_wait()
        table_grad[...] = tree(red_table, 4)[:prefix_count]
        finish_gather()
    out_copy.wait()
    in_copy.wait()


def run_block(comm, count, prefix_count, operands, weights_shape):
    length, width = operands[0].shape
    heads = width // HEAD_DIM
    hbm = pl.BlockSpec(memory_space=pl.ANY)
    vmem = pl.BlockSpec(memory_space=pltpu.VMEM)
    shape = jax.ShapeDtypeStruct
    scratch = [
        pltpu.VMEM(weights_shape, bf16),
        pltpu.VMEM((length, width), bf16),
        pltpu.VMEM((length, width), bf16),
        pltpu.VMEM((length, width), bf16),
        pltpu.VMEM((length, 3 * width), bf16),
        pltpu.VMEM((width, length), bf16),
        pltpu.VMEM((width, length), bf16),
        pltpu.VMEM((heads, length, length), bf16),
        pltpu.VMEM((length, length), f32),
        pltpu.VMEM((heads * PAD, width), bf16),
        pltpu.VMEM((heads * PAD, width), bf16),
        pltpu.VMEM((heads * PAD, length), f32),
        pltpu.VMEM((heads * PAD, length), bf16),
        pltpu.VMEM((heads * PAD, length), bf16),
        pltpu.VMEM((width, length), f32),
        pltpu.VMEM((length, width), f32),
        pltpu.VMEM((length, width), f32),
        pltpu.VMEM((length, width), f32),
        pltpu.VMEM((length, width), bf16),
        pltpu.VMEM((length, 3 * width), bf16),
        pltpu.VMEM((PAD, width), f32),
        pltpu.SemaphoreType.DMA((4,)),
        pltpu.SemaphoreType.DMA((12,)),
    ]
    outs = [shape((length, width), bf16), shape((length, width), f32)]
    out_specs = [hbm, hbm]
    if comm:
        hidden_units = operands[5].shape[1]
        kv_unit = operands[7].shape[1]
        in_specs = [hbm, hbm] + [vmem] * 7 + [hbm] * 4
        outs += [
            shape((prefix_count, width), f32),
            shape((width, hidden_units), f32),
            shape((1, hidden_units), f32),
            shape((hidden_units, kv_unit), f32),
            shape((1, kv_unit), f32),
            shape((prefix_count, kv_unit * count), f32),
        ]
        out_specs += [vmem] * 6
        scratch += [
            pltpu.VMEM((count, PAD, width // count), bf16),
            pltpu.VMEM((4, PAD, kv_unit), f32),
            pltpu.VMEM((count, PAD, kv_unit), f32),
            pltpu.VMEM((count, PAD, kv_unit), f32),
            pltpu.VMEM((count, PAD, kv_unit), f32),
            pltpu.VMEM((4, PAD, kv_unit), f32),
            pltpu.VMEM((count, PAD, hidden_units), f32),
            pltpu.VMEM((4, PAD, width), f32),
            pltpu.SemaphoreType.DMA((2,)),
            pltpu.SemaphoreType.DMA((2,)),
            pltpu.SemaphoreType.DMA((2,)),
            pltpu.SemaphoreType.DMA((4, 2)),
            pltpu.SemaphoreType.DMA((SLOTS,)),
            pltpu.SemaphoreType.DMA((SLOTS,)),
            pltpu.SemaphoreType.DMA((SLOTS, 4)),
            pltpu.SemaphoreType.DMA((SLOTS, 4)),
            pltpu.SemaphoreType.DMA((SLOTS, 4)),
            pltpu.SemaphoreType.DMA((SLOTS,)),
            pltpu.SemaphoreType.DMA((SLOTS, 5)),
        ]
        params = pltpu.CompilerParams(
            collective_id=0, has_side_effects=True, vmem_limit_bytes=66_500_000
        )
    else:
        in_specs = [hbm, hbm] + [vmem] * 3 + [hbm]
        outs += [shape((PAD, 2 * width), f32)]
        out_specs += [vmem]
        params = pltpu.CompilerParams(vmem_limit_bytes=66_500_000)
    return pl.pallas_call(
        functools.partial(block_kernel, comm, count, prefix_count),
        out_shape=tuple(outs),
        in_specs=in_specs,
        out_specs=tuple(out_specs),
        scratch_shapes=scratch,
        compiler_params=params,
    )(*operands)


def shards(
    tokens,
    segment_ids,
    cotangent,
    norm_in_gain,
    norm_in_shift,
    qkv_weight,
    qkv_bias,
    proj_weight,
    proj_bias,
    norm_mid_gain,
    norm_mid_shift,
    up_weight,
    up_bias,
    down_weight,
    down_bias,
    prefix_table,
    first_weight,
    first_bias,
    second_weight,
    second_bias,
):
    width = tokens.shape[-1]
    unit = qkv_weight.shape[0]
    count = width // unit
    reps = lax.axis_size("rep")
    prefix_count = prefix_table.shape[0]
    comm = count == 8 and reps == 4
    small = jnp.concatenate(
        [
            norm_in_gain,
            norm_in_shift,
            qkv_bias,
            proj_bias,
            norm_mid_gain,
            norm_mid_shift,
            up_bias,
            down_bias,
            jnp.zeros((3 * unit,), bf16),
        ]
    )
    if comm:
        operands = (
            tokens[0],
            cotangent[0],
            segment_ids,
            small.reshape(PAD, unit),
            prefix_table,
            first_weight,
            first_bias[None],
            second_weight,
            second_bias[None],
            qkv_weight,
            proj_weight,
            up_weight,
            down_weight,
        )
        (
            activations,
            input_grad,
            prefix_table_grad,
            first_weight_grad,
            first_bias_grad,
            second_weight_grad,
            second_bias_grad,
            prefix_kv,
        ) = run_block(True, count, prefix_count, operands, (count, 12 * unit, width))
        return (
            activations[None],
            input_grad[None],
            prefix_table_grad,
            first_weight_grad,
            first_bias_grad[0],
            second_weight_grad,
            second_bias_grad[0],
            prefix_kv,
        )
    local = jnp.concatenate(
        [qkv_weight[:, b * width : (b + 1) * width] for b in range(3)]
        + [proj_weight, down_weight]
        + [up_weight[:, b * width : (b + 1) * width] for b in range(4)],
        axis=0,
    )
    share = local.shape[0] // reps
    mine = lax.dynamic_slice_in_dim(local, lax.axis_index("rep") * share, share, axis=0)
    weights = lax.all_gather(mine, ("dp", "rep"), axis=0, tiled=True).reshape(
        count, local.shape[0], width
    )
    spread = lax.all_gather(small, "dp", axis=0)
    rows = []
    first = 0
    for number in (1, 1, 3, 1, 1, 1, 4, 1, 3):
        rows.append(spread[:, first : first + number * unit].reshape(number, width))
        first += number * unit
    vec = jnp.concatenate(rows, axis=0).astype(f32)
    hidden = jnp.tanh(
        jnp.dot(prefix_table, first_weight, preferred_element_type=f32) + first_bias.astype(f32)
    )
    hidden_low = hidden.astype(bf16)
    part = jnp.dot(hidden_low, second_weight, preferred_element_type=f32)
    part = lax.psum(part, "rep") + second_bias.astype(f32)
    prefix_kv = lax.all_gather(part, "dp", axis=1, tiled=True)
    prefix_low = jnp.pad(prefix_kv.astype(bf16), ((0, PAD - prefix_count), (0, 0)))
    activations, input_grad, prefix_grad = run_block(
        False,
        count,
        prefix_count,
        (tokens[0], cotangent[0], segment_ids, vec, prefix_low, weights),
        weights.shape,
    )
    prefix_grad = prefix_grad[:prefix_count]
    owned = lax.psum(
        lax.psum_scatter(prefix_grad, "dp", scatter_dimension=1, tiled=True), "rep"
    )
    hidden_values = hidden_low.astype(f32)
    second_weight_grad = jnp.dot(
        hidden_values.T, owned, precision=highest, preferred_element_type=f32
    )
    second_bias_grad = jnp.sum(owned, axis=0)
    hidden_part = jnp.dot(
        owned, second_weight.astype(f32).T, precision=highest, preferred_element_type=f32
    )
    grad_hidden = lax.psum(hidden_part, "dp")
    grad_inner = grad_hidden * (1.0 - hidden * hidden)
    first_weight_grad = jnp.dot(
        prefix_table.astype(f32).T, grad_inner, precision=highest, preferred_element_type=f32
    )
    first_bias_grad = jnp.sum(grad_inner, axis=0)
    table_part = jnp.dot(
        grad_inner, first_weight.astype(f32).T, precision=highest, preferred_element_type=f32
    )
    prefix_table_grad = lax.psum(table_part, "rep")
    return (
        activations[None],
        input_grad[None],
        prefix_table_grad,
        first_weight_grad,
        first_bias_grad,
        second_weight_grad,
        second_bias_grad,
        prefix_kv,
    )


def solution(mesh):
    in_specs = (
        P(("dp", "rep"), None, None),
        P(("dp", "rep"), None),
        P(("dp", "rep"), None, None),
        P("dp"),
        P("dp"),
        P("dp", None),
        P("dp"),
        P("dp", None),
        P("dp"),
        P("dp"),
        P("dp"),
        P("dp", None),
        P("dp"),
        P("dp", None),
        P("dp"),
        P(),
        P(None, "rep"),
        P("rep"),
        P("rep", "dp"),
        P("dp"),
    )
    out_specs = (
        P(("dp", "rep"), None, None),
        P(("dp", "rep"), None, None),
        P(),
        P(None, "rep"),
        P("rep"),
        P("rep", "dp"),
        P("dp"),
        P(),
    )
    return jax.shard_map(shards, mesh=mesh, in_specs=in_specs, out_specs=out_specs, check_vma=False)
```

time: 396 us -> 188 us (0.47)
  waiting for transfers between devices: 147 us -> 0 us
  blocking collectives: 126 us -> 0 us
  Pallas kernels: 84.5 us -> 167 us
  between operations: 14.3 us -> 0.68 us
    all_gather x1 -> x0, waiting for transfers between devices: 89.7 us -> none  [shards(): lax.all_gather(mine, ('dp', 'rep'), axis=0, tiled=True)]
    pallas_call x1, Pallas kernels: 84.5 us -> 167 us  [run_block(): pl.pallas_call(functools.partial(block_kernel, comm, count, prefix_count)...]
    psum x4 -> x0, blocking collectives: 75.9 us -> none  [the longest x1 28 us: shards(): grad_hidden = lax.psum(hidden_part, 'dp')]
    reduce_scatter x1 -> x0, waiting for transfers between devices: 57.2 us -> none  [shards(): lax.psum_scatter(prefix_grad, 'dp', scatter_dimension=1, tiled=True)]
    all_gather x2 -> x0, blocking collectives: 50.6 us -> none  [the longest x1 25.4 us: shards(): spread = lax.all_gather(small, 'dp', axis=0)]
    unnamed x41 -> x31, local copies, waits for them, and re-layouts: 12.4 us -> 18 us
  transfers between devices with their start and end apart: 2 -> 0, of which waited for: 2 -> 0; matrix products, arithmetic and copies ran while one was open for 1% -> 0% of each run, Pallas kernels for 0% -> 0%
where the time goes in v2:
time: 188 us
  Pallas kernels  167 us (89%)
  local copies, waits for them, and re-layouts  20.6 us (11%)
    pallas_call x1, Pallas kernels, run_block(): pl.pallas_call(functools.partial(block_kernel, comm, count, prefix_count)...  167 us
    unnamed x31, local copies, waits for them, and re-layouts  18 us

profile of v2, /device:TPU:1, one launch (start us, length us, event | category | flops | bytes accessed | tf_op | source)
XLA Modules:
  0.0 188.1 jit_solution(741189367897027301)
XLA Ops:
  0.6 1.2 broadcast_in_dim.16.refs_6_
  1.9 1.2 broadcast_in_dim.17.refs_8_
  3.1 0.8 dynamic-update-slice
  3.9 0.8 dynamic-update-slice.1
  4.7 0.9 dynamic-update-slice.2
  5.6 0.8 dynamic-update-slice.3
  6.4 0.8 dynamic-update-slice.4
  7.3 0.8 dynamic-update-slice.5
  8.1 0.9 dynamic-update-slice.6
  9.0 0.8 dynamic-update-slice.7
  9.8 0.2 dynamic-update-slice.8
  10.0 0.0 copy-start.4
  10.0 2.0 %copy.28.refs_5_ = bf16[1024,200]{1,0:T(8,128)(2,1)} copy(bf16[1024,200]{0,1:T(8,128)(2,1)} %param.36) | data formatting | bytes 819200 | tf_op args[16]
  12.0 0.0 copy-done.4
  12.0 166.8 %shard_map.251 = (bf16[512,1024]{1,0:T(8,128)(2,1)}, f32[512,1024]{1,0:T(8,128)}, f32[10,1024]{1,0:T(8,128)}, f32[1024,200]{1,0:T(8,128)}, f32[1,200]{1,0:T(1,12...) custom-call(bf16[512,1024]{1,0:T(8,128)(2,1)} %bitcast.8, bf16[512,1024]{1,0:T(8,128)(2,1)} %bitcast.9, ...), custom_call_target="tpu_custom_call" | custom-call | tf_op jit(solution)/shard_map/pallas_call | solution.py:778
  178.8 0.0 copy-start
  178.8 2.6 %copy.29 = f32[1024,200]{0,1:T(8,128)} copy(f32[1024,200]{1,0:T(8,128)} %get-tuple-element.27) | data formatting | bytes 1638400
  181.4 2.3 %copy.46 = bf16[1,512,1024]{2,1,0:T(8,128)(2,1)} copy(bf16[1,512,1024]{2,1,0:T(8,128)(2,1)} %bitcast.10) | data formatting | bytes 2097152
  183.7 0.0 copy-done
  183.7 0.0 copy-start.5
  183.7 0.0 copy-start.2
  183.7 1.3 copy.47
  185.0 0.0 copy-done.3
  185.0 0.6 copy.48
  185.6 0.0 copy-done.6
  185.6 0.6 copy.49
  186.2 0.0 copy-done.1
  186.2 0.7 copy.50
  186.9 0.0 copy-done.5
  186.9 0.6 copy.51
  187.5 0.0 copy-done.2
  187.5 0.7 copy.52
  (5 shorter events, 0.0 us)
Async XLA Ops:
  10.0 2.0 %copy-start.4 = (bf16[2048]{0:T(1024)(128)(2,1)}, bf16[2048]{0:T(1024)(128)(2,1)S(1)}, u32[]{:S(2)}) copy-start(bf16[2048]{0:T(1024)(128)(2,1)S(1)} %dynamic-update-slice.8) | copy-start | bytes 12292
  178.8 4.9 %copy-start = (f32[512,1024]{1,0:T(8,128)S(1)}, f32[512,1024]{1,0:T(8,128)}, u32[]{:S(2)}) copy-start(f32[512,1024]{1,0:T(8,128)} %get-tuple-element.17) | copy-start | bytes 6291460
  183.7 1.4 copy-start.3
  183.7 2.0 %copy-start.6 = (f32[1,200]{1,0:T(1,128)S(1)}, f32[1,200]{1,0:T(1,128)}, u32[]{:S(2)}) copy-start(f32[1,200]{1,0:T(1,128)} %get-tuple-element.20) | copy-start | bytes 2404
  183.7 2.5 %copy-start.1 = (f32[200,256]{1,0:T(8,128)S(1)}, f32[200,256]{1,0:T(8,128)}, u32[]{:S(2)}) copy-start(f32[200,256]{1,0:T(8,128)} %get-tuple-element.45) | copy-start | bytes 614404
  183.7 3.2 %copy-start.5 = (f32[1,256]{1,0:T(1,128)S(1)}, f32[1,256]{1,0:T(1,128)}, u32[]{:S(2)}) copy-start(f32[1,256]{1,0:T(1,128)} %get-tuple-element.22) | copy-start | bytes 3076
  183.7 3.8 %copy-start.2 = (f32[10,2048]{1,0:T(8,128)S(1)}, f32[10,2048]{1,0:T(8,128)}, u32[]{:S(2)}) copy-start(f32[10,2048]{1,0:T(8,128)} %get-tuple-element.47) | copy-start | bytes 245764
